TPU v7x, 256 devices: a whole 4x4x8 slice. The times are simulated.
256 devices in a mesh: blk: 64 (over y_hi, x, z), dp: 4 (over y_lo, core).
Axes of the slice: x: 4, y: 4 (y_hi: 2, y_lo: 2; y = y_hi * 2 + y_lo), z: 8, core: 2. Of those that a mesh axis runs over, the one named last changes fastest.
Arguments:
- x_rows: bfloat16 [65536, 2048], P('blk'), may hold values from -6 to 6
- grad_rows: bfloat16 [65536, 2048], P('blk'), may hold values from -3 to 3
- w_gate_up: bfloat16 [64, 2, 768, 2048], P('blk', None, 'dp'), may hold values from -0.125 to 0.125
- w_down: bfloat16 [64, 768, 2048], P('blk', 'dp'), may hold values from -0.21875 to 0.21875
- counts: int32 [64, 5], replicated, may hold values from 1 to 384, as said below
Outputs:
- grad_gate_up: float32 [64, 2, 768, 2048], P('blk', None, 'dp')
- grad_down: float32 [64, 768, 2048], P('blk', 'dp')
- grad_x: bfloat16 [65536, 2048], P('blk', 'dp')
Inputs may be any that keep to these rules, and one draw needn't show every extreme that they name: `counts`: on every device the 5 offsets take 3, 2, 1, 1 and 1 blocks of 128 rows, in an order drawn for each device, so the blocks fill all 1024 rows; an offset with k blocks has more than 128 * (k - 1) live rows; in every draw some device has an offset with exactly 384 live rows.
All inputs are finite; a program needn't handle non-finite values.
Results may differ from a plain program's by a relative error of at most 0.0095.
Values may be sent and summed in bfloat16 or wider, within the bound.
A program may use at most 192 MiB of HBM per device.

v0:
```python
import jax
import jax.numpy as jnp
from jax import lax
from jax.sharding import Mesh
from jax.sharding import PartitionSpec as P

HOPS = 4
BLOCK = 128
DP = ("dp_0", "dp_1")


def from_behind(block, axis, distance):
    devices = range(lax.axis_size(axis))
    route = [((i - distance) % len(devices), i) for i in devices]
    return lax.ppermute(block, axis, route)


def as_sent(shard):
    return jax.tree.map(lambda a: a.astype(jnp.bfloat16) if a.dtype == jnp.float32 else a, shard)


def own_block(pieces, axes, turns):
    inside = pieces.shape[1:]
    pieces = pieces.reshape(*(lax.axis_size(a) for a in axes), *inside)
    pieces = jnp.moveaxis(pieces, turns, range(len(axes))).reshape(-1, *inside)
    for k in turns:
        pieces = lax.psum_scatter(pieces, axes[k], scatter_dimension=0, tiled=True)
    return pieces[0]


def cut_along(shard, dim, count):
    before, after = (shard.shape[:dim], shard.shape[dim + 1 :])
    return jnp.moveaxis(shard.reshape(*before, count, -1, *after), dim, 0)


def sum_by_axis(shard, axes, turns, dim):
    count = lax.axis_size(axes)
    return own_block(cut_along(shard, dim, count), axes, turns)


def contract_last(lhs_array, rhs_array):
    return lax.dot_general(
        lhs_array, rhs_array, (((1,), (1,)), ((), ())), preferred_element_type=jnp.float32
    )


def contract_first(lhs_array, rhs_array):
    return lax.dot_general(
        lhs_array, rhs_array, (((0,), (0,)), ((), ())), preferred_element_type=jnp.float32
    )


def block_grads(weight_in, weight_out, rows_in, rows_cot):
    unit_count = weight_out.shape[0]
    projected = contract_last(rows_in, weight_in.reshape(2 * unit_count, weight_in.shape[2]))
    gate_pre = projected[:, :unit_count]
    up_pre = projected[:, unit_count:]
    sigmoid_gate = jax.nn.sigmoid(gate_pre)
    active = gate_pre * sigmoid_gate
    hidden = (active * up_pre).astype(jnp.bfloat16)
    hidden_grad = contract_last(rows_cot, weight_out)
    gate_gradient_rows = (
        hidden_grad * up_pre * sigmoid_gate * (1.0 + gate_pre * (1.0 - sigmoid_gate))
    ).astype(jnp.bfloat16)
    up_gradient_rows = (hidden_grad * active).astype(jnp.bfloat16)
    grad_in = jnp.stack(
        [contract_first(gate_gradient_rows, rows_in), contract_first(up_gradient_rows, rows_in)]
    )
    grad_out = contract_first(hidden, rows_cot)
    row_grad = jnp.dot(gate_gradient_rows, weight_in[0], preferred_element_type=jnp.float32)
    row_grad = row_grad + jnp.dot(
        up_gradient_rows, weight_in[1], preferred_element_type=jnp.float32
    )
    return (grad_in, grad_out, row_grad)


def process_rows(
    weight_in, weight_out, row_source, cot_source, row_start, row_count, acc_in, acc_out, row_grads
):
    block_count = (row_count + BLOCK - 1) // BLOCK

    def one_block(block_idx, totals):
        sum_in, sum_out, grads_now = totals
        row_first = row_start + block_idx * BLOCK
        rows_in = lax.dynamic_slice_in_dim(row_source, row_first, BLOCK, 0)
        rows_cot = lax.dynamic_slice_in_dim(cot_source, row_first, BLOCK, 0)
        live_rows = block_idx * BLOCK + jnp.arange(BLOCK, dtype=jnp.int32) < row_count
        rows_cot = jnp.where(live_rows[:, None], rows_cot, jnp.zeros((), jnp.bfloat16))
        grad_in, grad_out, row_grad = block_grads(weight_in, weight_out, rows_in, rows_cot)
        grads_now = lax.dynamic_update_slice_in_dim(grads_now, row_grad, row_first, 0)
        return (sum_in + grad_in, sum_out + grad_out, grads_now)

    return lax.fori_loop(0, block_count, one_block, (acc_in, acc_out, row_grads))


def on_device(x_rows, grad_rows, w_gate_up, w_down, counts):
    weight_in = w_gate_up[0]
    weight_out = w_down[0]
    total_rows = x_rows.shape[0]
    features = weight_out.shape[1]
    position = lax.axis_index("blk")
    own_counts = lax.dynamic_index_in_dim(counts, position, 0, keepdims=False)
    blocks = (own_counts + BLOCK - 1) // BLOCK
    starts = (jnp.cumsum(blocks) - blocks) * BLOCK
    empty_in = jnp.zeros(weight_in.shape, jnp.float32)
    empty_out = jnp.zeros(weight_out.shape, jnp.float32)
    rows_grad = jnp.zeros((total_rows, features), jnp.float32)
    held_panel = (weight_in, weight_out)
    shares = []
    for travel in range(HOPS + 1):
        if travel > 0:
            held_panel = from_behind((held_panel[0], held_panel[1]), "blk", 1)
        grad_in, grad_out, rows_grad = process_rows(
            held_panel[0],
            held_panel[1],
            x_rows,
            grad_rows,
            starts[travel],
            own_counts[travel],
            empty_in,
            empty_out,
            rows_grad,
        )
        shares.append((grad_in, grad_out))
    carried = shares[HOPS]
    for travel in range(HOPS - 1, -1, -1):
        returned_homeward = from_behind((as_sent(carried[0]), as_sent(carried[1])), "blk", -1)
        carried = (
            returned_homeward[0] + shares[travel][0],
            returned_homeward[1] + shares[travel][1],
        )
    total_in, output_total_sum = carried
    reduced = sum_by_axis(rows_grad.astype(jnp.bfloat16), DP, (1, 0), 1).astype(jnp.float32)
    return (total_in[None], output_total_sum[None], reduced.astype(jnp.bfloat16))


def solution(mesh):
    finer = Mesh(mesh.devices.reshape(mesh.shape["blk"], 2, 2), ("blk", "dp_0", "dp_1"))
    placed = (P("blk", None), P("blk", None), P("blk", None, DP, None), P("blk", DP, None), P())
    return jax.shard_map(
        on_device,
        mesh=finer,
        in_specs=placed,
        out_specs=(P("blk", None, DP, None), P("blk", DP, None), P("blk", DP)),
        check_vma=False,
    )
```

profile of v0, /device:TPU:247, one launch (start us, length us, event | category | flops | bytes accessed | tf_op | source)
XLA Modules:
  0.0 580.1 jit_solution(3801145930772125733)
XLA Ops:
  10.4 49.3 %collective-permute-done = bf16[192,2048]{1,0:T(8,128)(2,1)} collective-permute-done((bf16[192,2048]{1,0:T(8,128)(2,1)}, bf16[192,2048]{1,0:T(8,128)(2,1)}, u32[]{:S(2)}, u32[]{:S(2)}) %collective-permute-start) | collective-permute-done | bytes 786464 | tf_op jit(solution)/shard_map/ppermute | solution.py:15
  59.7 6.1 %collective-permute-start.2 = (bf16[192,2048]{1,0:T(8,128)(2,1)}, bf16[192,2048]{1,0:T(8,128)(2,1)}, u32[]{:S(2)}, u32[]{:S(2)}) collective-permute-start(bf16[192,2048]{1,0:T(8,128)(2,1)} %collective-permute-done), channel_id=1, source_target_pairs={{252,0},{0,4},{4,8},{8,12},{12,16},{16,20},{20,24},{24,28},{28,32}... | collective-permute-start | bytes 2359304 | tf_op jit(solution)/shard_map/ppermute | solution.py:15
  65.8 2.5 broadcast_in_dim.66
  68.3 2.0 broadcast_in_dim.64.clone
  70.5 16.0 %while.70 = (s32[]{:T(128)}, f32[2,192,2048]{2,1,0:T(8,128)}, f32[192,2048]{1,0:T(8,128)S(1)}, bf16[1024,2048]{1,0:T(8,128)(2,1)}, s32[]{:T(128)}, /*index=5*/s3...) while((s32[]{:T(128)}, f32[2,192,2048]{2,1,0:T(8,128)}, ...), condition=%wide.region_2.3_spmd, body=%wide.region_1.2_spmd.sunk | while | flops 808788224 | bytes 55149248 | solution.py:93
  71.2 1.7 fusion.209
  75.1 1.6 convolution_bitcast_fusion.21
  80.9 4.0 dynamic_update_slice.20
  91.3 19.7 %while.71 = (s32[]{:T(128)}, f32[2,192,2048]{2,1,0:T(8,128)S(1)}, f32[192,2048]{1,0:T(8,128)}, bf16[1024,2048]{1,0:T(8,128)(2,1)}, s32[]{:T(128)}, /*index=5*/s3...) while((s32[]{:T(128)}, f32[2,192,2048]{2,1,0:T(8,128)S(1)}, ...), condition=%wide.region_4.5_spmd, body=%wide.region_3.4_spmd.sunk | while | flops 808788224 | bytes 26837608 | solution.py:93
  91.9 2.2 fusion.222
  94.7 1.8 multiply_convert_fusion.33
  101.6 2.3 convolution_add_fusion.23
  103.9 4.0 dynamic_update_slice.21
  107.9 3.2 convolution_add_fusion.22
  111.0 29.4 %collective-permute-done.4 = bf16[192,2048]{1,0:T(8,128)(2,1)} collective-permute-done((bf16[192,2048]{1,0:T(8,128)(2,1)}, bf16[192,2048]{1,0:T(8,128)(2,1)}, u32[]{:S(2)}, u32[]{:S(2)}) %collective-permute-start.4) | collective-permute-done | bytes 786464 | tf_op jit(solution)/shard_map/ppermute | solution.py:15
  140.4 6.0 %collective-permute-start.6 = (bf16[192,2048]{1,0:T(8,128)(2,1)}, bf16[192,2048]{1,0:T(8,128)(2,1)}, u32[]{:S(2)}, u32[]{:S(2)}) collective-permute-start(bf16[192,2048]{1,0:T(8,128)(2,1)} %collective-permute-done.4), channel_id=1, source_target_pairs={{252,0},{0,4},{4,8},{8,12},{12,16},{16,20},{20,24},{24,28},{28,32}... | collective-permute-start | bytes 2359304 | tf_op jit(solution)/shard_map/ppermute | solution.py:15
  146.5 3.7 collective-permute-start.5
  150.2 2.1 broadcast_in_dim.64.clone.2
  153.7 38.5 %while.72 = (s32[]{:T(128)}, f32[2,192,2048]{2,1,0:T(8,128)}, f32[192,2048]{1,0:T(8,128)}, bf16[1024,2048]{1,0:T(8,128)(2,1)}, s32[]{:T(128)}, /*index=5*/s32[]{...) while((s32[]{:T(128)}, f32[2,192,2048]{2,1,0:T(8,128)}, ...), condition=%wide.region_6.7_spmd, body=%wide.region_5.6_spmd.sunk | while | flops 808788224 | bytes 64586456 | solution.py:93
  154.2 2.2 fusion.235
  157.0 1.8 multiply_convert_fusion.35
  158.7 1.6 convolution_bitcast_fusion.25
  162.7 2.0 fusion.236
  166.4 3.8 dynamic_update_slice.22
  173.5 2.2 fusion.235
  176.2 1.8 multiply_convert_fusion.35
  182.0 2.0 fusion.236
  185.6 3.8 dynamic_update_slice.22
  192.2 3.0 collective-permute-done.5
  195.2 18.5 %collective-permute-start.7 = (bf16[2,192,2048]{2,1,0:T(8,128)(2,1)}, bf16[2,192,2048]{2,1,0:T(8,128)(2,1)S(1)}, u32[]{:S(2)}, u32[]{:S(2)}) collective-permute-start(bf16[2,192,2048]{2,1,0:T(8,128)(2,1)} %collective-permute-done.5), channel_id=1, source_target_pairs={{252,0},{0,4},{4,8},{8,12},{12,16},{16,20},{20,24},{24,28},{28,32}... | collective-permute-start | bytes 4718600 | tf_op jit(solution)/shard_map/ppermute | solution.py:15
  213.6 2.0 broadcast_in_dim.64.clone.3
  215.8 56.9 %while.73 = (s32[]{:T(128)}, f32[2,192,2048]{2,1,0:T(8,128)}, f32[192,2048]{1,0:T(8,128)S(1)}, bf16[1024,2048]{1,0:T(8,128)(2,1)}, s32[]{:T(128)}, /*index=5*/s3...) while((s32[]{:T(128)}, f32[2,192,2048]{2,1,0:T(8,128)}, ...), condition=%wide.region_8.9_spmd, body=%wide.region_7.8_spmd.sunk | while | flops 808788224 | bytes 52003488 | solution.py:93
  216.6 2.2 fusion.248
  219.4 1.8 multiply_convert_fusion.37
  225.2 2.0 fusion.249
  227.2 2.3 convolution_add_fusion.27
  229.4 4.0 dynamic_update_slice.23
  235.5 2.2 fusion.248
  238.3 1.8 multiply_convert_fusion.37
  244.1 2.0 fusion.249
  246.1 2.3 convolution_add_fusion.27
  248.3 4.0 dynamic_update_slice.23
  254.4 2.2 fusion.248
  257.2 1.8 multiply_convert_fusion.37
  262.9 2.0 fusion.249
  265.0 2.3 convolution_add_fusion.27
  267.2 4.0 dynamic_update_slice.23
  273.9 2.0 broadcast_in_dim.64
  276.1 15.4 %while.74 = (s32[]{:T(128)}, f32[2,192,2048]{2,1,0:T(8,128)}, f32[192,2048]{1,0:T(8,128)S(1)}, bf16[1024,2048]{1,0:T(8,128)(2,1)}, s32[]{:T(128)}, /*index=5*/s3...) while((s32[]{:T(128)}, f32[2,192,2048]{2,1,0:T(8,128)}, ...), condition=%wide.region_10.11_spmd, body=%wide.region_9.10_spmd.sunk | while | flops 808788224 | bytes 52003488 | solution.py:93
  276.7 1.6 fusion.261
  278.9 1.8 multiply_convert_fusion.39
  286.5 3.5 dynamic_update_slice.24
  291.5 7.0 %copy.38 = bf16[1024,2048]{0,1:T(8,128)(2,1)} copy(bf16[1024,2048]{1,0:T(8,128)(2,1)} %get-tuple-element.322) | data formatting | bytes 8388608 | tf_op jit(solution)/shard_map/while | solution.py:93
  298.5 6.2 %copy.40 = bf16[2,2,1024,512]{3,2,1,0:T(8,128)(2,1)} copy(bf16[2,2,1024,512]{2,3,0,1:T(8,128)(2,1)} %bitcast.238) | data formatting | bytes 8388608 | tf_op jit(solution)/shard_map/transpose | solution.py:25
  304.8 1.8 copy-done.3
  307.0 38.0 %collective-permute-done.8 = bf16[2,192,2048]{2,1,0:T(8,128)(2,1)S(1)} collective-permute-done((bf16[2,192,2048]{2,1,0:T(8,128)(2,1)S(1)}, bf16[2,192,2048]{2,1,0:T(8,128)(2,1)S(1)}, u32[]{:S(2)}, u32[]{:S(2)}) %collective-permute-start.8) | collective-permute-done | bytes 1572896 | tf_op jit(solution)/shard_map/ppermute | solution.py:15
  346.5 53.3 %collective-permute-done.9 = bf16[2,192,2048]{2,1,0:T(8,128)(2,1)S(1)} collective-permute-done((bf16[2,192,2048]{2,1,0:T(8,128)(2,1)S(1)}, bf16[2,192,2048]{2,1,0:T(8,128)(2,1)S(1)}, u32[]{:S(2)}, u32[]{:S(2)}) %collective-permute-start.9) | collective-permute-done | bytes 1572896 | tf_op jit(solution)/shard_map/ppermute | solution.py:15
  400.7 16.0 %collective-permute-done.12 = bf16[192,2048]{1,0:T(8,128)(2,1)S(1)} collective-permute-done((bf16[192,2048]{1,0:T(8,128)(2,1)S(1)}, bf16[192,2048]{1,0:T(8,128)(2,1)S(1)}, u32[]{:S(2)}, u32[]{:S(2)}) %collective-permute-start.12) | collective-permute-done | bytes 786464 | tf_op jit(solution)/shard_map/ppermute | solution.py:15
  417.8 49.6 %collective-permute-done.13 = bf16[192,2048]{1,0:T(8,128)(2,1)} collective-permute-done((bf16[192,2048]{1,0:T(8,128)(2,1)}, bf16[192,2048]{1,0:T(8,128)(2,1)}, u32[]{:S(2)}, u32[]{:S(2)}) %collective-permute-start.13) | collective-permute-done | bytes 786464 | tf_op jit(solution)/shard_map/ppermute | solution.py:15
  468.8 2.1 add_convert_fusion
  471.0 18.2 %collective-permute-done.14 = bf16[192,2048]{1,0:T(8,128)(2,1)S(1)} collective-permute-done((bf16[192,2048]{1,0:T(8,128)(2,1)S(1)}, bf16[192,2048]{1,0:T(8,128)(2,1)S(1)}, u32[]{:S(2)}, u32[]{:S(2)}) %collective-permute-start.14) | collective-permute-done | bytes 786464 | tf_op jit(solution)/shard_map/ppermute | solution.py:15
  489.5 50.3 %collective-permute-done.15 = bf16[192,2048]{1,0:T(8,128)(2,1)S(1)} collective-permute-done((bf16[192,2048]{1,0:T(8,128)(2,1)S(1)}, bf16[192,2048]{1,0:T(8,128)(2,1)S(1)}, u32[]{:S(2)}, u32[]{:S(2)}) %collective-permute-start.15) | collective-permute-done | bytes 786464 | tf_op jit(solution)/shard_map/ppermute | solution.py:15
  541.1 2.1 add_bitcast_fusion
  543.2 30.0 %reduce-scatter.5.cloned.1.call-done = bf16[1,1024,512]{2,1,0:T(8,128)(2,1)} async-done(((bf16[2,1024,512]{2,1,0:T(8,128)(2,1)}), bf16[1,1024,512]{2,1,0:T(8,128)(2,1)}) %reduce-scatter.5.cloned.1.call-update) | async-done | bytes 1048592 | tf_op jit(solution)/shard_map/reduce_scatter | solution.py:27
  (156 shorter events, 70.6 us)
Async XLA Ops:
  7.2 410.6 %reduce-scatter.3.cloned.1.call-start = ((), (), s32[]{:S(2)}) async-start(), calls=%async_computation.2 | async-start | bytes 6291456 | tf_op jit(solution)/shard_map/reduce_scatter | solution.py:27
  7.2 81.6 %collective-permute-start.1 = (bf16[2,192,2048]{2,1,0:T(8,128)(2,1)}, bf16[2,192,2048]{2,1,0:T(8,128)(2,1)}, u32[]{:S(2)}, u32[]{:S(2)}) collective-permute-start(bf16[2,192,2048]{2,1,0:T(8,128)(2,1)} %bitcast.232), channel_id=1, source_target_pairs={{252,0},{0,4},{4,8},{8,12},{12,16},{16,20},{20,24},{24,28},{28,32}... | collective-permute-start | bytes 4718600 | tf_op jit(solution)/shard_map/ppermute | solution.py:15
  7.3 52.4 %collective-permute-start = (bf16[192,2048]{1,0:T(8,128)(2,1)}, bf16[192,2048]{1,0:T(8,128)(2,1)}, u32[]{:S(2)}, u32[]{:S(2)}) collective-permute-start(bf16[192,2048]{1,0:T(8,128)(2,1)} %bitcast.240), channel_id=1, source_target_pairs={{252,0},{0,4},{4,8},{8,12},{12,16},{16,20},{20,24},{24,28},{28,32}... | collective-permute-start | bytes 2359304 | tf_op jit(solution)/shard_map/ppermute | solution.py:15
  59.7 29.2 %collective-permute-start.2 = (bf16[192,2048]{1,0:T(8,128)(2,1)}, bf16[192,2048]{1,0:T(8,128)(2,1)}, u32[]{:S(2)}, u32[]{:S(2)}) collective-permute-start(bf16[192,2048]{1,0:T(8,128)(2,1)} %collective-permute-done), channel_id=1, source_target_pairs={{252,0},{0,4},{4,8},{8,12},{12,16},{16,20},{20,24},{24,28},{28,32}... | collective-permute-start | bytes 2359304 | tf_op jit(solution)/shard_map/ppermute | solution.py:15
  68.3 2.2 copy-start
  71.2 2.4 copy-start.25
  75.1 3.0 copy-start.12
  79.1 1.8 copy-start.13
  86.4 3.2 copy-start.23
  88.8 57.6 %collective-permute-start.3 = (bf16[2,192,2048]{2,1,0:T(8,128)(2,1)}, bf16[2,192,2048]{2,1,0:T(8,128)(2,1)}, u32[]{:S(2)}, u32[]{:S(2)}) collective-permute-start(bf16[2,192,2048]{2,1,0:T(8,128)(2,1)} %collective-permute-done.1), channel_id=1, source_target_pairs={{252,0},{0,4},{4,8},{8,12},{12,16},{16,20},{20,24},{24,28},{28,32}... | collective-permute-start | bytes 4718600 | tf_op jit(solution)/shard_map/ppermute | solution.py:15
  88.9 51.5 %collective-permute-start.4 = (bf16[192,2048]{1,0:T(8,128)(2,1)}, bf16[192,2048]{1,0:T(8,128)(2,1)}, u32[]{:S(2)}, u32[]{:S(2)}) collective-permute-start(bf16[192,2048]{1,0:T(8,128)(2,1)} %collective-permute-done.2), channel_id=1, source_target_pairs={{252,0},{0,4},{4,8},{8,12},{12,16},{16,20},{20,24},{24,28},{28,32}... | collective-permute-start | bytes 2359304 | tf_op jit(solution)/shard_map/ppermute | solution.py:15
  111.0 42.6 %copy-start.4 = (f32[2,192,2048]{2,1,0:T(8,128)}, f32[2,192,2048]{2,1,0:T(8,128)S(1)}, u32[]{:S(2)}) copy-start(f32[2,192,2048]{2,1,0:T(8,128)S(1)} %get-tuple-element.315) | copy-start | bytes 9437188
  140.4 132.3 %collective-permute-start.6 = (bf16[192,2048]{1,0:T(8,128)(2,1)}, bf16[192,2048]{1,0:T(8,128)(2,1)}, u32[]{:S(2)}, u32[]{:S(2)}) collective-permute-start(bf16[192,2048]{1,0:T(8,128)(2,1)} %collective-permute-done.4), channel_id=1, source_target_pairs={{252,0},{0,4},{4,8},{8,12},{12,16},{16,20},{20,24},{24,28},{28,32}... | collective-permute-start | bytes 2359304 | tf_op jit(solution)/shard_map/ppermute | solution.py:15
  146.5 48.7 %collective-permute-start.5 = (bf16[2,192,2048]{2,1,0:T(8,128)(2,1)}, bf16[2,192,2048]{2,1,0:T(8,128)(2,1)}, u32[]{:S(2)}, u32[]{:S(2)}) collective-permute-start(bf16[2,192,2048]{2,1,0:T(8,128)(2,1)} %collective-permute-done.3), channel_id=1, source_target_pairs={{252,0},{0,4},{4,8},{8,12},{12,16},{16,20},{20,24},{24,28},{28,32}... | collective-permute-start | bytes 4718600 | tf_op jit(solution)/shard_map/ppermute | solution.py:15
  158.7 3.0 copy-start.6
  162.7 3.6 copy-start.7
  164.8 5.4 copy-start.18
  171.7 1.2 copy-start.19
  178.0 3.0 copy-start.6
  182.0 3.6 copy-start.7
  184.0 5.4 copy-start.18
  190.9 1.2 copy-start.19
  195.2 77.6 %collective-permute-start.7 = (bf16[2,192,2048]{2,1,0:T(8,128)(2,1)}, bf16[2,192,2048]{2,1,0:T(8,128)(2,1)S(1)}, u32[]{:S(2)}, u32[]{:S(2)}) collective-permute-start(bf16[2,192,2048]{2,1,0:T(8,128)(2,1)} %collective-permute-done.5), channel_id=1, source_target_pairs={{252,0},{0,4},{4,8},{8,12},{12,16},{16,20},{20,24},{24,28},{28,32}... | collective-permute-start | bytes 4718600 | tf_op jit(solution)/shard_map/ppermute | solution.py:15
  221.2 3.0 copy-start.9
  225.1 4.3 copy-start.10
  240.1 3.0 copy-start.9
  244.0 4.3 copy-start.10
  258.9 3.0 copy-start.9
  262.9 4.3 copy-start.10
  272.7 1.1 copy-start.21
  280.7 3.0 copy-start.1
  284.7 1.8 copy-start.2
  291.5 7.0 %copy-start.15 = (f32[192,2048]{1,0:T(8,128)}, f32[192,2048]{1,0:T(8,128)S(1)}, u32[]{:S(2)}) copy-start(f32[192,2048]{1,0:T(8,128)S(1)} %get-tuple-element.317) | copy-start | bytes 4718596
  304.7 1.9 copy-start.3
  304.8 268.5 %reduce-scatter.5.cloned.1.call-start = ((), (), s32[]{:S(2)}) async-start(), calls=%async_computation.3 | async-start | bytes 3145728 | tf_op jit(solution)/shard_map/reduce_scatter | solution.py:27
  306.6 38.3 %copy-start.11 = (f32[2,192,2048]{2,1,0:T(8,128)S(1)}, f32[2,192,2048]{2,1,0:T(8,128)}, u32[]{:S(2)}) copy-start(f32[2,192,2048]{2,1,0:T(8,128)} %get-tuple-element.313) | copy-start | bytes 9437188
  306.9 38.1 %collective-permute-start.8 = (bf16[2,192,2048]{2,1,0:T(8,128)(2,1)S(1)}, bf16[2,192,2048]{2,1,0:T(8,128)(2,1)S(1)}, u32[]{:S(2)}, u32[]{:S(2)}) collective-permute-start(bf16[2,192,2048]{2,1,0:T(8,128)(2,1)S(1)} %convert_element_type.98), channel_id=1, source_target_pairs={{4,0},{8,4},{12,8},{16,12},{20,16},{24,20},{28,24},{32,28},{36,32}... | collective-permute-start | bytes 4718600 | tf_op jit(solution)/shard_map/ppermute | solution.py:15
  344.9 1.4 copy-start.16
  344.9 54.9 %copy-start.8 = (f32[2,192,2048]{2,1,0:T(8,128)S(1)}, f32[2,192,2048]{2,1,0:T(8,128)}, u32[]{:S(2)}) copy-start(f32[2,192,2048]{2,1,0:T(8,128)} %get-tuple-element.314) | copy-start | bytes 9437188
  345.5 54.4 %collective-permute-start.9 = (bf16[2,192,2048]{2,1,0:T(8,128)(2,1)S(1)}, bf16[2,192,2048]{2,1,0:T(8,128)(2,1)S(1)}, u32[]{:S(2)}, u32[]{:S(2)}) collective-permute-start(bf16[2,192,2048]{2,1,0:T(8,128)(2,1)S(1)} %add_convert_fusion.2), channel_id=1, source_target_pairs={{4,0},{8,4},{12,8},{16,12},{20,16},{24,20},{28,24},{32,28},{36,32}... | collective-permute-start | bytes 4718600 | tf_op jit(solution)/shard_map/ppermute | solution.py:15
  346.4 70.2 %collective-permute-start.12 = (bf16[192,2048]{1,0:T(8,128)(2,1)S(1)}, bf16[192,2048]{1,0:T(8,128)(2,1)S(1)}, u32[]{:S(2)}, u32[]{:S(2)}) collective-permute-start(bf16[192,2048]{1,0:T(8,128)(2,1)S(1)} %convert_element_type.106), channel_id=1, source_target_pairs={{4,0},{8,4},{12,8},{16,12},{20,16},{24,20},{28,24},{32,28},{36,32}... | collective-permute-start | bytes 2359304 | tf_op jit(solution)/shard_map/ppermute | solution.py:15
  399.8 16.9 %copy-start.22 = (f32[192,2048]{1,0:T(8,128)S(1)}, f32[192,2048]{1,0:T(8,128)}, u32[]{:S(2)}) copy-start(f32[192,2048]{1,0:T(8,128)} %copy-done.21) | copy-start | bytes 4718596
  400.3 68.4 %collective-permute-start.10 = (bf16[2,192,2048]{2,1,0:T(8,128)(2,1)S(1)}, bf16[2,192,2048]{2,1,0:T(8,128)(2,1)}, u32[]{:S(2)}, u32[]{:S(2)}) collective-permute-start(bf16[2,192,2048]{2,1,0:T(8,128)(2,1)S(1)} %add_convert_fusion.1), channel_id=1, source_target_pairs={{4,0},{8,4},{12,8},{16,12},{20,16},{24,20},{28,24},{32,28},{36,32}... | collective-permute-start | bytes 4718600 | tf_op jit(solution)/shard_map/ppermute | solution.py:15
  416.7 50.7 %copy-start.20 = (f32[192,2048]{1,0:T(8,128)S(1)}, f32[192,2048]{1,0:T(8,128)}, u32[]{:S(2)}) copy-start(f32[192,2048]{1,0:T(8,128)} %get-tuple-element.319) | copy-start | bytes 4718596
  417.7 49.6 %collective-permute-start.13 = (bf16[192,2048]{1,0:T(8,128)(2,1)}, bf16[192,2048]{1,0:T(8,128)(2,1)}, u32[]{:S(2)}, u32[]{:S(2)}) collective-permute-start(bf16[192,2048]{1,0:T(8,128)(2,1)} %add_convert_fusion.5), channel_id=1, source_target_pairs={{4,0},{8,4},{12,8},{16,12},{20,16},{24,20},{28,24},{32,28},{36,32}... | collective-permute-start | bytes 2359304 | tf_op jit(solution)/shard_map/ppermute | solution.py:15
  417.8 51.0 %copy-start.5 = (f32[2,192,2048]{2,1,0:T(8,128)S(1)}, f32[2,192,2048]{2,1,0:T(8,128)}, u32[]{:S(2)}) copy-start(f32[2,192,2048]{2,1,0:T(8,128)} %copy-done.4) | copy-start | bytes 9437188
  468.7 20.5 %collective-permute-start.14 = (bf16[192,2048]{1,0:T(8,128)(2,1)S(1)}, bf16[192,2048]{1,0:T(8,128)(2,1)S(1)}, u32[]{:S(2)}, u32[]{:S(2)}) collective-permute-start(bf16[192,2048]{1,0:T(8,128)(2,1)S(1)} %add_convert_fusion.4), channel_id=1, source_target_pairs={{4,0},{8,4},{12,8},{16,12},{20,16},{24,20},{28,24},{32,28},{36,32}... | collective-permute-start | bytes 2359304 | tf_op jit(solution)/shard_map/ppermute | solution.py:15
  468.8 20.4 %copy-start.17 = (f32[192,2048]{1,0:T(8,128)S(1)}, f32[192,2048]{1,0:T(8,128)}, u32[]{:S(2)}) copy-start(f32[192,2048]{1,0:T(8,128)} %get-tuple-element.320) | copy-start | bytes 4718596
  470.9 68.8 %copy-start.24 = (f32[192,2048]{1,0:T(8,128)S(1)}, f32[192,2048]{1,0:T(8,128)}, u32[]{:S(2)}) copy-start(f32[192,2048]{1,0:T(8,128)} %copy-done.23) | copy-start | bytes 4718596
  470.9 70.2 %collective-permute-start.11 = (bf16[2,192,2048]{2,1,0:T(8,128)(2,1)S(1)}, bf16[2,192,2048]{2,1,0:T(8,128)(2,1)S(1)}, u32[]{:S(2)}, u32[]{:S(2)}) collective-permute-start(bf16[2,192,2048]{2,1,0:T(8,128)(2,1)S(1)} %add_convert_fusion), channel_id=1, source_target_pairs={{4,0},{8,4},{12,8},{16,12},{20,16},{24,20},{28,24},{32,28},{36,32}... | collective-permute-start | bytes 4718600 | tf_op jit(solution)/shard_map/ppermute | solution.py:15
  489.4 51.8 %copy-start.14 = (f32[2,192,2048]{2,1,0:T(8,128)S(1)}, f32[2,192,2048]{2,1,0:T(8,128)}, u32[]{:S(2)}) copy-start(f32[2,192,2048]{2,1,0:T(8,128)} %get-tuple-element.316) | copy-start | bytes 9437188
  489.4 50.4 %collective-permute-start.15 = (bf16[192,2048]{1,0:T(8,128)(2,1)S(1)}, bf16[192,2048]{1,0:T(8,128)(2,1)S(1)}, u32[]{:S(2)}, u32[]{:S(2)}) collective-permute-start(bf16[192,2048]{1,0:T(8,128)(2,1)S(1)} %add_convert_fusion.3), channel_id=1, source_target_pairs={{4,0},{8,4},{12,8},{16,12},{20,16},{24,20},{28,24},{32,28},{36,32}... | collective-permute-start | bytes 2359304 | tf_op jit(solution)/shard_map/ppermute | solution.py:15
Sparse Core Ops, SparseCore 0:
  304.9 58.1 reduce-scatter.2
  417.9 155.3 reduce-scatter.4
where the time goes:
time: 583 us; the launch traced here: 580 us
  waiting for transfers between devices  337 us (58%)
  matrix products  95.3 us (16%)
  local copies, waits for them, and re-layouts  66.1 us (11%)
  starting transfers between devices  36.1 us (6%)
  other arithmetic  22.6 us (4%)
  between operations  17.4 us (3%)
    ppermute x16, waiting for transfers between devices, from_behind(): return lax.ppermute(block, axis, route)  307 us
    dot_general x24, matrix products, contract_first(): lax.dot_general(lhs_array, rhs_array, (((0,), (0,)), ((), ())), preferred...  37.6 us
    ppermute x16, starting transfers between devices, from_behind(): return lax.ppermute(block, axis, route)  36 us
    dynamic_update_slice x8, local copies, waits for them, and re-layouts, one_block(): lax.dynamic_update_slice_in_dim(grads_now, row_grad, row_first, 0)  31.1 us
    dot_general x16, matrix products, contract_last(): lax.dot_general(lhs_array, rhs_array, (((1,), (1,)), ((), ())), preferred...  30.3 us
    reduce_scatter x2, waiting for transfers between devices, own_block(): pieces = lax.psum_scatter(pieces, axes[k], scatter_dimension=0, tiled=True)  30 us
    dot_general x8, matrix products, block_grads(): jnp.dot(up_gradient_rows, weight_in[1], preferred_element_type=jnp.float32)  15.1 us
    dot_general x8, matrix products, block_grads(): jnp.dot(gate_gradient_rows, weight_in[0], preferred_element_type=jnp.floa...  12.2 us
  transfers between devices with their start and end apart: 18, of which 10 were waited for; matrix products, arithmetic and copies ran while one was open for 25% of the time, Pallas kernels for 0%

commit v1 on v0

v1 whole, which is shorter than its diff:
```python
import jax
import jax.numpy as jnp
from jax import lax
from jax.experimental import pallas as pl
from jax.experimental.pallas import tpu as pltpu
from jax.sharding import Mesh
from jax.sharding import PartitionSpec as P

HOPS = 4
BLOCK = 128
SLOTS = 3
DP = ("dp_0", "dp_1")
MESH = pl.DeviceIdType.MESH
UNITS = SLOTS * (HOPS + 1)
REMOTE = SLOTS * HOPS


def contract_last(lhs, rhs):
    return lax.dot_general(lhs, rhs, (((1,), (1,)), ((), ())), preferred_element_type=jnp.float32)


def contract_first(lhs, rhs):
    return lax.dot_general(lhs, rhs, (((0,), (0,)), ((), ())), preferred_element_type=jnp.float32)


def kernel(
    n_blk,
    counts,
    x_hbm,
    g_hbm,
    w_in,
    w_out,
    grad_in,
    grad_out,
    grad_x,
    x_quarter,
    g_quarter,
    staged,
    full,
    pieces,
    pieces_in,
    half_out,
    half_in,
    home_out,
    home,
    load_sem,
    z_send,
    z_recv,
    y_send,
    y_recv,
    c_send,
    c_recv,
    d_send,
    d_recv,
    p_send,
    p_recv,
    h_send,
    h_recv,
    r_send,
    r_recv,
):
    b, y, c = lax.axis_index("blk"), lax.axis_index("dp_0"), lax.axis_index("dp_1")
    unit_count = w_out.shape[0]
    quarter = x_quarter.shape[2]

    def around(steps):
        return lax.rem(b + steps + n_blk, n_blk)

    y_peer, c_peer = (b, 1 - y, c), (b, y, 1 - c)

    def cols(y_of, c_of):
        return pl.ds(pl.multiple_of((2 * y_of + c_of) * quarter, quarter), quarter)

    own = cols(y, c)
    loads = [
        pltpu.make_async_copy(x_hbm.at[:, :, own], x_quarter, load_sem.at[0]),
        pltpu.make_async_copy(g_hbm.at[:, :, own], g_quarter, load_sem.at[1]),
    ]
    for k in range(SLOTS):
        loads.append(pltpu.make_async_copy(x_hbm.at[k], full.at[k, 0], load_sem.at[2 + 2 * k]))
        loads.append(pltpu.make_async_copy(g_hbm.at[k], full.at[k, 1], load_sem.at[3 + 2 * k]))
    for load in loads:
        load.start()

    barrier = pltpu.get_barrier_semaphore()
    for o in range(1, HOPS + 1):
        for steps in (o, -o):
            pl.semaphore_signal(barrier, 1, device_id=(around(steps), y, c), device_id_type=MESH)
    pl.semaphore_signal(barrier, 1, device_id=y_peer, device_id_type=MESH)
    pl.semaphore_signal(barrier, 1, device_id=c_peer, device_id_type=MESH)

    live_of = [counts[b, o] for o in range(HOPS + 1)]
    blocks = [lax.shift_right_logical(n + (BLOCK - 1), 7) for n in live_of]
    starts = [jnp.int32(0)]
    for o in range(HOPS):
        starts.append(starts[o] + blocks[o])
    row_id = lax.broadcasted_iota(jnp.int32, (BLOCK, 1), 0)

    def remote(src, dst, send, recv, target):
        return pltpu.make_async_remote_copy(
            src_ref=src, dst_ref=dst, send_sem=send, recv_sem=recv, device_id=target, device_id_type=MESH
        )

    def z_copy(j, o):
        return remote(
            staged.at[j],
            full.at[SLOTS + j, :, :, own],
            z_send.at[j],
            z_recv.at[j],
            (around(-o), y, c),
        )

    loads[0].wait()
    loads[1].wait()
    pl.semaphore_wait(barrier, 2 * HOPS + 2)
    for j in range(REMOTE):
        k, o = j // HOPS, 1 + j % HOPS
        block = jnp.clip(starts[o] + jnp.minimum(k, blocks[o] - 1), 0, x_quarter.shape[0] - 1)
        staged[j, 0] = x_quarter[block]
        live = row_id < live_of[o] - k * BLOCK
        staged[j, 1] = jnp.where(live, g_quarter[block], jnp.zeros((), jnp.bfloat16))
        z_copy(j, o).start()

    for load in loads[2:]:
        load.wait()
    for k in range(SLOTS):
        live = row_id < live_of[0] - k * BLOCK
        full[k, 1] = jnp.where(live, full[k, 1], jnp.zeros((), jnp.bfloat16))
    grad_in[...] = jnp.zeros_like(grad_in)
    grad_out[...] = jnp.zeros_like(grad_out)

    def y_copy(j):
        part = full.at[SLOTS + j, :, :, own]
        return remote(part, part, y_send.at[j], y_recv.at[j], y_peer)

    def c_copy(j):
        part = full.at[SLOTS + j, :, :, own]
        return remote(part, part, c_send.at[j], c_recv.at[j], c_peer)

    def d_copy(j):
        part = full.at[SLOTS + j, :, :, cols(1 - y, c)]
        return remote(part, part, d_send.at[j], d_recv.at[j], c_peer)

    def p_copy(u):
        return remote(pieces.at[u, 1 - c], pieces_in.at[u], p_send.at[u], p_recv.at[u], c_peer)

    def h_copy(u):
        return remote(half_out.at[u], half_in.at[u], h_send.at[u], h_recv.at[u], y_peer)

    def r_copy(j):
        o = 1 + lax.rem(j, HOPS)
        return remote(home_out.at[j], home.at[SLOTS + j], r_send.at[j], r_recv.at[j], (around(o), y, c))

    def compute(u):
        rows_in, rows_cot = full[u, 0], full[u, 1]
        projected = contract_last(rows_in, w_in[...])
        gate_pre, up_pre = projected[:, :unit_count], projected[:, unit_count:]
        sigmoid_gate = jax.nn.sigmoid(gate_pre)
        active = gate_pre * sigmoid_gate
        hidden = (active * up_pre).astype(jnp.bfloat16)
        hidden_grad = contract_last(rows_cot, w_out[...])
        gate_grad = hidden_grad * up_pre * sigmoid_gate * (1.0 + gate_pre * (1.0 - sigmoid_gate))
        both = jnp.concatenate([gate_grad, hidden_grad * active], axis=1).astype(jnp.bfloat16)
        for q in range(4):
            pieces[u, q % 2, q // 2] = jnp.dot(
                both, w_in[:, q * quarter : (q + 1) * quarter], preferred_element_type=jnp.float32
            ).astype(jnp.bfloat16)
        p_copy(u).start()
        grad_in[...] += contract_first(both, rows_in)
        grad_out[...] += contract_first(hidden, rows_cot)

    def partial_sum(u, y_of):
        return pieces[u, c, y_of].astype(jnp.float32) + pieces_in[u, y_of].astype(jnp.float32)

    def step(s, carry):
        @pl.when((s >= 2) & (s < UNITS + 2))
        def _():
            u = s - 2

            @pl.when(u >= SLOTS)
            def _():
                c_copy(u - SLOTS).wait_recv()
                d_copy(u - SLOTS).wait_recv()

            compute(u)

        @pl.when((s >= 3) & (s < UNITS + 3))
        def _():
            u = s - 3
            p_copy(u).wait_recv()
            half_out[u] = partial_sum(u, 1 - y).astype(jnp.bfloat16)
            h_copy(u).start()

        @pl.when((s >= 4) & (s < UNITS + 4))
        def _():
            u = s - 4
            h_copy(u).wait_recv()
            total = (partial_sum(u, y) + half_in[u].astype(jnp.float32)).astype(jnp.bfloat16)

            @pl.when(u < SLOTS)
            def _():
                home[u] = total

            @pl.when(u >= SLOTS)
            def _():
                home_out[u - SLOTS] = total
                r_copy(u - SLOTS).start()

        @pl.when((s >= 1 + SLOTS) & (s < UNITS + 1))
        def _():
            j = s - 1 - SLOTS
            y_copy(j).wait_recv()
            d_copy(j).start()

        @pl.when((s >= SLOTS) & (s < UNITS))
        def _():
            j = s - SLOTS
            z_copy(j, 1).wait_recv()
            y_copy(j).start()
            c_copy(j).start()

        return carry

    lax.fori_loop(0, UNITS + 4, step, 0)

    def drain(j, carry):
        r_copy(j).wait_recv()
        z_copy(j, 1).wait_send()
        y_copy(j).wait_send()
        c_copy(j).wait_send()
        d_copy(j).wait_send()
        r_copy(j).wait_send()
        return carry

    lax.fori_loop(0, REMOTE, drain, 0)

    def drain_sums(u, carry):
        p_copy(u).wait_send()
        h_copy(u).wait_send()
        return carry

    lax.fori_loop(0, UNITS, drain_sums, 0)

    for p in range(grad_x.shape[0] // BLOCK):
        unit = jnp.int32(0)
        for o in range(HOPS + 1):
            k = p - starts[o]
            here = k if o == 0 else SLOTS + k * HOPS + o - 1
            unit = jnp.where((k >= 0) & (k < blocks[o]), here, unit)
        grad_x[pl.ds(p * BLOCK, BLOCK), :] = home[jnp.clip(unit, 0, UNITS - 1)]


def on_device(x_rows, grad_rows, w_gate_up, w_down, counts):
    rows, features = x_rows.shape
    units = w_down.shape[1]
    quarter = features // 4
    vmem = pl.BlockSpec(memory_space=pltpu.VMEM)
    held = pl.BlockSpec(memory_space=pl.ANY)
    b16, f32 = jnp.bfloat16, jnp.float32
    dma = pltpu.SemaphoreType.DMA
    grad_in, grad_out, grad_x = pl.pallas_call(
        lambda *refs: kernel(lax.axis_size("blk"), *refs),
        name="experts_backward",
        out_shape=(
            jax.ShapeDtypeStruct((2 * units, features), f32),
            jax.ShapeDtypeStruct((units, features), f32),
            jax.ShapeDtypeStruct((rows, quarter), b16),
        ),
        in_specs=[pl.BlockSpec(memory_space=pltpu.SMEM), held, held, vmem, vmem],
        out_specs=(vmem, vmem, vmem),
        scratch_shapes=[
            pltpu.VMEM((rows // BLOCK, BLOCK, quarter), b16),
            pltpu.VMEM((rows // BLOCK, BLOCK, quarter), b16),
            pltpu.VMEM((REMOTE, 2, BLOCK, quarter), b16),
            pltpu.VMEM((UNITS, 2, BLOCK, features), b16),
            pltpu.VMEM((UNITS, 2, 2, BLOCK, quarter), b16),
            pltpu.VMEM((UNITS, 2, BLOCK, quarter), b16),
            pltpu.VMEM((UNITS, BLOCK, quarter), b16),
            pltpu.VMEM((UNITS, BLOCK, quarter), b16),
            pltpu.VMEM((REMOTE, BLOCK, quarter), b16),
            pltpu.VMEM((UNITS, BLOCK, quarter), b16),
            dma((2 + 2 * SLOTS,)),
            *[dma((REMOTE,))] * 8,
            *[dma((UNITS,))] * 4,
            *[dma((REMOTE,))] * 2,
        ],
        compiler_params=pltpu.CompilerParams(
            collective_id=0, has_side_effects=True, vmem_limit_bytes=60 * 1024 * 1024
        ),
    )(
        counts,
        x_rows.reshape(-1, BLOCK, features),
        grad_rows.reshape(-1, BLOCK, features),
        w_gate_up.reshape(2 * units, features),
        w_down.reshape(units, features),
    )
    return (grad_in.reshape(1, 2, units, features), grad_out[None], grad_x)


def solution(mesh):
    finer = Mesh(mesh.devices.reshape(mesh.shape["blk"], 2, 2), ("blk", "dp_0", "dp_1"))
    placed = (P("blk", None), P("blk", None), P("blk", None, DP, None), P("blk", DP, None), P())
    return jax.shard_map(
        on_device,
        mesh=finer,
        in_specs=placed,
        out_specs=(P("blk", None, DP, None), P("blk", DP, None), P("blk", DP)),
        check_vma=False,
    )
```

time: 583 us -> 216 us (0.37)
  the two profiles are of different devices: /device:TPU:247 before, /device:TPU:96 now
where the time goes in v1:
time: 216 us
  Pallas kernels  207 us (96%)
  local copies, waits for them, and re-layouts  8.18 us (4%)
    pallas_call x1, Pallas kernels, on_device(): pl.pallas_call(lambda *refs: kernel(lax.axis_size('blk'), *refs), name='e...  207 us
    unnamed x8, local copies, waits for them, and re-layouts  8.18 us

profile of v1, /device:TPU:96, one launch (start us, length us, event | category | flops | bytes accessed | tf_op | source)
XLA Modules:
  0.0 216.2 jit_solution(9288890551256326516)
XLA Ops:
  0.6 1.4 copy.8.refs_0_
  2.0 207.3 %experts_backward.1 = (f32[384,2048]{1,0:T(8,128)}, f32[192,2048]{1,0:T(8,128)}, bf16[1024,512]{1,0:T(8,128)(2,1)}) custom-call(s32[64,5]{1,0:T(8,128)} %copy.8.refs_0_, bf16[8,128,2048]{2,1,0:T(8,128)(2,1)} %bitcast.6, bf16[8,128,2048]{2,1,0:T(8,128)(2,1)} %bitcast.7, bf16[384,2048]{1,0:T(8,128)(2,1)} %bitcast.10, bf16[192,2048]{1,0:T(8,128)(2,1)} %bitcast.11), custom_call_target="tpu_custom_call" | custom-call | tf_op jit(solution)/shard_map/experts_backward/pallas_call | solution.py:261
  209.4 0.0 copy-start
  209.4 4.0 %copy.12 = f32[1,2,192,2048]{3,2,1,0:T(8,128)} copy(f32[1,2,192,2048]{3,2,1,0:T(8,128)} %bitcast.8) | data formatting | bytes 6291456
  213.4 0.0 copy-done
  213.4 0.0 copy-start.1
  213.4 1.1 copy.13
  214.6 0.6 copy-done.1
  215.2 1.0 copy.14
Async XLA Ops:
  209.4 4.0 %copy-start = (f32[192,2048]{1,0:T(8,128)S(1)}, f32[192,2048]{1,0:T(8,128)}, u32[]{:S(2)}) copy-start(f32[192,2048]{1,0:T(8,128)} %get-tuple-element.7) | copy-start | bytes 4718596
  213.4 1.8 copy-start.1

commit v2 on v1

--- a/solution.py
+++ b/solution.py
@@ -23,9 +23,25 @@
     return lax.dot_general(lhs, rhs, (((0,), (0,)), ((), ())), preferred_element_type=jnp.float32)
 
 
+HALF_WAY = HOPS
+COLUMN = 8
+IN_FLIGHT = 4
+
+
+def offset_of(j):
+    turn, i = j // HOPS, j % HOPS
+    last = turn // (SLOTS - 1)
+    return (1 - last) * (i + 1 + i // 2 - 2 * (i // 3)) + last * (HOPS - i)
+
+
+UNIT_OF = {(offset_of(j), j // HOPS): j for j in range(REMOTE)}
+DIRECT = [j for j in range(REMOTE) if offset_of(j) < HALF_WAY]
+RELAYED = [j for j in range(REMOTE) if offset_of(j) == HALF_WAY]
+
+
 def kernel(
     n_blk,
-    counts,
+    counts_hbm,
     x_hbm,
     g_hbm,
     w_in,
@@ -36,6 +52,7 @@
     x_quarter,
     g_quarter,
     staged,
+    passing,
     full,
     pieces,
     pieces_in,
@@ -43,9 +60,12 @@
     half_in,
     home_out,
     home,
+    counts,
     load_sem,
     z_send,
     z_recv,
+    n_send,
+    n_recv,
     y_send,
     y_recv,
     c_send,
@@ -66,7 +86,13 @@
     def around(steps):
         return lax.rem(b + steps + n_blk, n_blk)
 
+    def up(position, steps):
+        level = lax.rem(position, COLUMN)
+        return position - level + lax.rem(level + steps, COLUMN)
+
     y_peer, c_peer = (b, 1 - y, c), (b, y, 1 - c)
+    relay_to = (up(b, 1), y, c)
+    passed_to = (lax.rem(up(b, COLUMN - 1) - HALF_WAY + n_blk, n_blk), y, c)
 
     def cols(y_of, c_of):
         return pl.ds(pl.multiple_of((2 * y_of + c_of) * quarter, quarter), quarter)
@@ -79,16 +105,18 @@
     for k in range(SLOTS):
         loads.append(pltpu.make_async_copy(x_hbm.at[k], full.at[k, 0], load_sem.at[2 + 2 * k]))
         loads.append(pltpu.make_async_copy(g_hbm.at[k], full.at[k, 1], load_sem.at[3 + 2 * k]))
+    loads.append(pltpu.make_async_copy(counts_hbm, counts, load_sem.at[2 + 2 * SLOTS]))
     for load in loads:
         load.start()
 
     barrier = pltpu.get_barrier_semaphore()
-    for o in range(1, HOPS + 1):
-        for steps in (o, -o):
-            pl.semaphore_signal(barrier, 1, device_id=(around(steps), y, c), device_id_type=MESH)
-    pl.semaphore_signal(barrier, 1, device_id=y_peer, device_id_type=MESH)
-    pl.semaphore_signal(barrier, 1, device_id=c_peer, device_id_type=MESH)
-
+    senders = [(around(steps), y, c) for steps in (1, 2, 3, -1, -2, -3, -4)]
+    senders += [(up(b, COLUMN - 1), y, c), (up(around(HALF_WAY), 1), y, c), y_peer, c_peer]
+    for sender in senders:
+        pl.semaphore_signal(barrier, 1, device_id=sender, device_id_type=MESH)
+
+    for load in (loads[0], loads[1], loads[-1]):
+        load.wait()
     live_of = [counts[b, o] for o in range(HOPS + 1)]
     blocks = [lax.shift_right_logical(n + (BLOCK - 1), 7) for n in live_of]
     starts = [jnp.int32(0)]
@@ -101,27 +129,34 @@
             src_ref=src, dst_ref=dst, send_sem=send, recv_sem=recv, device_id=target, device_id_type=MESH
         )
 
-    def z_copy(j, o):
-        return remote(
-            staged.at[j],
-            full.at[SLOTS + j, :, :, own],
-            z_send.at[j],
-            z_recv.at[j],
-            (around(-o), y, c),
-        )
-
-    loads[0].wait()
-    loads[1].wait()
-    pl.semaphore_wait(barrier, 2 * HOPS + 2)
-    for j in range(REMOTE):
-        k, o = j // HOPS, 1 + j % HOPS
+    def z_copy(j, target):
+        return remote(staged.at[j], full.at[SLOTS + j, :, :, own], z_send.at[j], z_recv.at[j], target)
+
+    def start_direct(j):
+        z_copy(j, (around(-offset_of(j)), y, c)).start()
+
+    def relay_copy(k):
+        j = UNIT_OF[HALF_WAY, k]
+        return remote(staged.at[j], passing.at[k], z_send.at[j], n_recv.at[k], relay_to)
+
+    def pass_copy(k):
+        j = UNIT_OF[HALF_WAY, k]
+        return remote(passing.at[k], full.at[SLOTS + j, :, :, own], n_send.at[k], z_recv.at[j], passed_to)
+
+    for count, j in enumerate(RELAYED[:1] + DIRECT[:1] + RELAYED[1:] + DIRECT[1:]):
+        k, o = j // HOPS, offset_of(j)
         block = jnp.clip(starts[o] + jnp.minimum(k, blocks[o] - 1), 0, x_quarter.shape[0] - 1)
         staged[j, 0] = x_quarter[block]
         live = row_id < live_of[o] - k * BLOCK
         staged[j, 1] = jnp.where(live, g_quarter[block], jnp.zeros((), jnp.bfloat16))
-        z_copy(j, o).start()
-
-    for load in loads[2:]:
+        if count == 0:
+            pl.semaphore_wait(barrier, len(senders))
+        if o == HALF_WAY:
+            relay_copy(k).start()
+        elif j in DIRECT[:IN_FLIGHT]:
+            start_direct(j)
+
+    for load in loads[2:-1]:
         load.wait()
     for k in range(SLOTS):
         live = row_id < live_of[0] - k * BLOCK
@@ -148,7 +183,7 @@
         return remote(half_out.at[u], half_in.at[u], h_send.at[u], h_recv.at[u], y_peer)
 
     def r_copy(j):
-        o = 1 + lax.rem(j, HOPS)
+        o = offset_of(j)
         return remote(home_out.at[j], home.at[SLOTS + j], r_send.at[j], r_recv.at[j], (around(o), y, c))
 
     def compute(u):
@@ -173,59 +208,75 @@
         return pieces[u, c, y_of].astype(jnp.float32) + pieces_in[u, y_of].astype(jnp.float32)
 
     def step(s, carry):
-        @pl.when((s >= 2) & (s < UNITS + 2))
+        for i, j in enumerate(DIRECT[IN_FLIGHT:]):
+
+            @pl.when(s == i + 2)
+            def _():
+                z_copy(DIRECT[i], y_peer).wait_send()
+                start_direct(j)
+
+        @pl.when(s >= 2)
         def _():
             u = s - 2
+            h_copy(u).wait_recv()
+            total = (partial_sum(u, y) + half_in[u].astype(jnp.float32)).astype(jnp.bfloat16)
+
+            @pl.when(u < SLOTS)
+            def _():
+                home[u] = total
 
             @pl.when(u >= SLOTS)
             def _():
-                c_copy(u - SLOTS).wait_recv()
-                d_copy(u - SLOTS).wait_recv()
-
-            compute(u)
-
-        @pl.when((s >= 3) & (s < UNITS + 3))
-        def _():
-            u = s - 3
+                home_out[u - SLOTS] = total
+                r_copy(u - SLOTS).start()
+
+        @pl.when((s >= 1) & (s < UNITS + 1))
+        def _():
+            u = s - 1
             p_copy(u).wait_recv()
             half_out[u] = partial_sum(u, 1 - y).astype(jnp.bfloat16)
             h_copy(u).start()
 
-        @pl.when((s >= 4) & (s < UNITS + 4))
-        def _():
-            u = s - 4
-            h_copy(u).wait_recv()
-            total = (partial_sum(u, y) + half_in[u].astype(jnp.float32)).astype(jnp.bfloat16)
-
-            @pl.when(u < SLOTS)
-            def _():
-                home[u] = total
-
-            @pl.when(u >= SLOTS)
-            def _():
-                home_out[u - SLOTS] = total
-                r_copy(u - SLOTS).start()
-
-        @pl.when((s >= 1 + SLOTS) & (s < UNITS + 1))
-        def _():
-            j = s - 1 - SLOTS
+        @pl.when(s < UNITS)
+        def _():
+            @pl.when(s >= SLOTS)
+            def _():
+                c_copy(s - SLOTS).wait_recv()
+                d_copy(s - SLOTS).wait_recv()
+
+            compute(s)
+
+        @pl.when((s + 1 >= SLOTS) & (s + 1 < UNITS))
+        def _():
+            j = s + 1 - SLOTS
             y_copy(j).wait_recv()
             d_copy(j).start()
 
-        @pl.when((s >= SLOTS) & (s < UNITS))
-        def _():
-            j = s - SLOTS
-            z_copy(j, 1).wait_recv()
+        for k in range(SLOTS):
+
+            @pl.when(s == k)
+            def _():
+                relay_copy(k).wait_recv()
+                pass_copy(k).start()
+
+        @pl.when((s + 2 >= SLOTS) & (s + 2 < UNITS))
+        def _():
+            j = s + 2 - SLOTS
+            z_copy(j, y_peer).wait_recv()
             y_copy(j).start()
             c_copy(j).start()
 
         return carry
 
-    lax.fori_loop(0, UNITS + 4, step, 0)
+    lax.fori_loop(0, UNITS + 2, step, 0)
+
+    for j in RELAYED + DIRECT[-IN_FLIGHT:]:
+        z_copy(j, y_peer).wait_send()
+    for k in range(SLOTS):
+        pass_copy(k).wait_send()
 
     def drain(j, carry):
         r_copy(j).wait_recv()
-        z_copy(j, 1).wait_send()
         y_copy(j).wait_send()
         c_copy(j).wait_send()
         d_copy(j).wait_send()
@@ -244,9 +295,9 @@
     for p in range(grad_x.shape[0] // BLOCK):
         unit = jnp.int32(0)
         for o in range(HOPS + 1):
-            k = p - starts[o]
-            here = k if o == 0 else SLOTS + k * HOPS + o - 1
-            unit = jnp.where((k >= 0) & (k < blocks[o]), here, unit)
+            for k in range(SLOTS):
+                here = k if o == 0 else SLOTS + UNIT_OF[o, k]
+                unit = jnp.where((starts[o] + k == p) & (k < blocks[o]), here, unit)
         grad_x[pl.ds(p * BLOCK, BLOCK), :] = home[jnp.clip(unit, 0, UNITS - 1)]
 
 
@@ -266,12 +317,13 @@
             jax.ShapeDtypeStruct((units, features), f32),
             jax.ShapeDtypeStruct((rows, quarter), b16),
         ),
-        in_specs=[pl.BlockSpec(memory_space=pltpu.SMEM), held, held, vmem, vmem],
+        in_specs=[held, held, held, vmem, vmem],
         out_specs=(vmem, vmem, vmem),
         scratch_shapes=[
             pltpu.VMEM((rows // BLOCK, BLOCK, quarter), b16),
             pltpu.VMEM((rows // BLOCK, BLOCK, quarter), b16),
             pltpu.VMEM((REMOTE, 2, BLOCK, quarter), b16),
+            pltpu.VMEM((SLOTS, 2, BLOCK, quarter), b16),
             pltpu.VMEM((UNITS, 2, BLOCK, features), b16),
             pltpu.VMEM((UNITS, 2, 2, BLOCK, quarter), b16),
             pltpu.VMEM((UNITS, 2, BLOCK, quarter), b16),
@@ -279,8 +331,11 @@
             pltpu.VMEM((UNITS, BLOCK, quarter), b16),
             pltpu.VMEM((REMOTE, BLOCK, quarter), b16),
             pltpu.VMEM((UNITS, BLOCK, quarter), b16),
-            dma((2 + 2 * SLOTS,)),
-            *[dma((REMOTE,))] * 8,
+            pltpu.SMEM(counts.shape, counts.dtype),
+            dma((3 + 2 * SLOTS,)),
+            *[dma((REMOTE,))] * 2,
+            *[dma((SLOTS,))] * 2,
+            *[dma((REMOTE,))] * 6,
             *[dma((UNITS,))] * 4,
             *[dma((REMOTE,))] * 2,
         ],

time: 216 us -> 217 us (level)
  the two profiles are of different devices: /device:TPU:96 before, /device:TPU:24 now
where the time goes in v2:
time: 217 us; the launch traced here: 216 us
  Pallas kernels  208 us (96%)
  local copies, waits for them, and re-layouts  8.18 us (4%)
    pallas_call x1, Pallas kernels, on_device(): pl.pallas_call(lambda *refs: kernel(lax.axis_size('blk'), *refs), name='e...  208 us
    unnamed x8, local copies, waits for them, and re-layouts  8.18 us

profile of v2, /device:TPU:24, one launch (start us, length us, event | category | flops | bytes accessed | tf_op | source)
XLA Modules:
  0.0 216.3 jit_solution(2186554604887005415)
XLA Ops:
  0.6 1.4 copy.8.refs_0_
  2.0 207.5 %experts_backward.1 = (f32[384,2048]{1,0:T(8,128)}, f32[192,2048]{1,0:T(8,128)}, bf16[1024,512]{1,0:T(8,128)(2,1)}) custom-call(s32[64,5]{1,0:T(8,128)} %copy.8.refs_0_, bf16[8,128,2048]{2,1,0:T(8,128)(2,1)} %bitcast.6, bf16[8,128,2048]{2,1,0:T(8,128)(2,1)} %bitcast.7, bf16[384,2048]{1,0:T(8,128)(2,1)} %bitcast.10, bf16[192,2048]{1,0:T(8,128)(2,1)} %bitcast.11), custom_call_target="tpu_custom_call" | custom-call | tf_op jit(solution)/shard_map/experts_backward/pallas_call | solution.py:312
  209.5 0.0 copy-start
  209.5 4.0 %copy.12 = f32[1,2,192,2048]{3,2,1,0:T(8,128)} copy(f32[1,2,192,2048]{3,2,1,0:T(8,128)} %bitcast.8) | data formatting | bytes 6291456
  213.6 0.0 copy-done
  213.6 0.0 copy-start.1
  213.6 1.1 copy.13
  214.7 0.6 copy-done.1
  215.4 1.0 copy.14
Async XLA Ops:
  209.5 4.0 %copy-start = (f32[192,2048]{1,0:T(8,128)S(1)}, f32[192,2048]{1,0:T(8,128)}, u32[]{:S(2)}) copy-start(f32[192,2048]{1,0:T(8,128)} %get-tuple-element.7) | copy-start | bytes 4718596
  213.6 1.8 copy-start.1

commit v3 on v2

--- a/solution.py
+++ b/solution.py
@@ -25,6 +25,7 @@
 
 HALF_WAY = HOPS
 COLUMN = 8
+HALF = 32
 IN_FLIGHT = 4
 
 
@@ -81,43 +82,50 @@
 ):
     b, y, c = lax.axis_index("blk"), lax.axis_index("dp_0"), lax.axis_index("dp_1")
     unit_count = w_out.shape[0]
-    quarter = x_quarter.shape[2]
-
-    def around(steps):
-        return lax.rem(b + steps + n_blk, n_blk)
+    quarter = x_quarter.shape[3]
 
     def up(position, steps):
         level = lax.rem(position, COLUMN)
         return position - level + lax.rem(level + steps, COLUMN)
 
+    def behind(position, o):
+        crossed = 1 - (lax.rem(position, HALF) - o + HALF) // HALF
+        return (lax.rem(position - o + n_blk, n_blk), y + crossed * (1 - 2 * y), c)
+
+    def ahead(position, o):
+        crossed = (lax.rem(position, HALF) + o) // HALF
+        return (lax.rem(position + o, n_blk), y + crossed * (1 - 2 * y), c)
+
     y_peer, c_peer = (b, 1 - y, c), (b, y, 1 - c)
     relay_to = (up(b, 1), y, c)
-    passed_to = (lax.rem(up(b, COLUMN - 1) - HALF_WAY + n_blk, n_blk), y, c)
+    passed_to = behind(up(b, COLUMN - 1), HALF_WAY)
 
     def cols(y_of, c_of):
         return pl.ds(pl.multiple_of((2 * y_of + c_of) * quarter, quarter), quarter)
 
     own = cols(y, c)
-    loads = [
-        pltpu.make_async_copy(x_hbm.at[:, :, own], x_quarter, load_sem.at[0]),
-        pltpu.make_async_copy(g_hbm.at[:, :, own], g_quarter, load_sem.at[1]),
-    ]
+    loads = []
+    for y_of in range(2):
+        for held, source in ((x_quarter, x_hbm), (g_quarter, g_hbm)):
+            copy = pltpu.make_async_copy(source.at[:, :, cols(y_of, c)], held.at[y_of], load_sem.at[len(loads)])
+            loads.append(copy)
     for k in range(SLOTS):
-        loads.append(pltpu.make_async_copy(x_hbm.at[k], full.at[k, 0], load_sem.at[2 + 2 * k]))
-        loads.append(pltpu.make_async_copy(g_hbm.at[k], full.at[k, 1], load_sem.at[3 + 2 * k]))
-    loads.append(pltpu.make_async_copy(counts_hbm, counts, load_sem.at[2 + 2 * SLOTS]))
+        for held, source in ((0, x_hbm), (1, g_hbm)):
+            loads.append(pltpu.make_async_copy(source.at[k], full.at[k, held], load_sem.at[len(loads)]))
+    loads.append(pltpu.make_async_copy(counts_hbm, counts, load_sem.at[len(loads)]))
     for load in loads:
         load.start()
 
     barrier = pltpu.get_barrier_semaphore()
-    senders = [(around(steps), y, c) for steps in (1, 2, 3, -1, -2, -3, -4)]
-    senders += [(up(b, COLUMN - 1), y, c), (up(around(HALF_WAY), 1), y, c), y_peer, c_peer]
+    senders = [ahead(b, o) for o in range(1, HALF_WAY)] + [behind(b, o) for o in range(1, HOPS + 1)]
+    home_of_far = ahead(b, HALF_WAY)
+    senders += [(up(b, COLUMN - 1), y, c), (up(home_of_far[0], 1), home_of_far[1], c), y_peer, c_peer]
     for sender in senders:
         pl.semaphore_signal(barrier, 1, device_id=sender, device_id_type=MESH)
 
-    for load in (loads[0], loads[1], loads[-1]):
+    for load in (*loads[:4], loads[-1]):
         load.wait()
-    live_of = [counts[b, o] for o in range(HOPS + 1)]
+    live_of = [counts[o, b] for o in range(HOPS + 1)]
     blocks = [lax.shift_right_logical(n + (BLOCK - 1), 7) for n in live_of]
     starts = [jnp.int32(0)]
     for o in range(HOPS):
@@ -130,10 +138,11 @@
         )
 
     def z_copy(j, target):
-        return remote(staged.at[j], full.at[SLOTS + j, :, :, own], z_send.at[j], z_recv.at[j], target)
+        part = full.at[SLOTS + j, :, :, cols(target[1], c)]
+        return remote(staged.at[j], part, z_send.at[j], z_recv.at[j], target)
 
     def start_direct(j):
-        z_copy(j, (around(-offset_of(j)), y, c)).start()
+        z_copy(j, behind(b, offset_of(j))).start()
 
     def relay_copy(k):
         j = UNIT_OF[HALF_WAY, k]
@@ -141,14 +150,16 @@
 
     def pass_copy(k):
         j = UNIT_OF[HALF_WAY, k]
-        return remote(passing.at[k], full.at[SLOTS + j, :, :, own], n_send.at[k], z_recv.at[j], passed_to)
+        part = full.at[SLOTS + j, :, :, cols(passed_to[1], c)]
+        return remote(passing.at[k], part, n_send.at[k], z_recv.at[j], passed_to)
 
     for count, j in enumerate(RELAYED[:1] + DIRECT[:1] + RELAYED[1:] + DIRECT[1:]):
         k, o = j // HOPS, offset_of(j)
-        block = jnp.clip(starts[o] + jnp.minimum(k, blocks[o] - 1), 0, x_quarter.shape[0] - 1)
-        staged[j, 0] = x_quarter[block]
+        block = jnp.clip(starts[o] + jnp.minimum(k, blocks[o] - 1), 0, x_quarter.shape[1] - 1)
+        y_of = behind(b, o)[1]
+        staged[j, 0] = x_quarter[y_of, block]
         live = row_id < live_of[o] - k * BLOCK
-        staged[j, 1] = jnp.where(live, g_quarter[block], jnp.zeros((), jnp.bfloat16))
+        staged[j, 1] = jnp.where(live, g_quarter[y_of, block], jnp.zeros((), jnp.bfloat16))
         if count == 0:
             pl.semaphore_wait(barrier, len(senders))
         if o == HALF_WAY:
@@ -156,7 +167,7 @@
         elif j in DIRECT[:IN_FLIGHT]:
             start_direct(j)
 
-    for load in loads[2:-1]:
+    for load in loads[4:-1]:
         load.wait()
     for k in range(SLOTS):
         live = row_id < live_of[0] - k * BLOCK
@@ -183,8 +194,11 @@
         return remote(half_out.at[u], half_in.at[u], h_send.at[u], h_recv.at[u], y_peer)
 
     def r_copy(j):
-        o = offset_of(j)
-        return remote(home_out.at[j], home.at[SLOTS + j], r_send.at[j], r_recv.at[j], (around(o), y, c))
+        return remote(home_out.at[j], home.at[SLOTS + j], r_send.at[j], r_recv.at[j], ahead(b, offset_of(j)))
+
+    def finished_by(u):
+        away = (u + UNITS - SLOTS) // UNITS
+        return ahead(b, away * offset_of(u - away * SLOTS))[1]
 
     def compute(u):
         rows_in, rows_cot = full[u, 0], full[u, 1]
@@ -219,7 +233,7 @@
         def _():
             u = s - 2
             h_copy(u).wait_recv()
-            total = (partial_sum(u, y) + half_in[u].astype(jnp.float32)).astype(jnp.bfloat16)
+            total = (partial_sum(u, finished_by(u)) + half_in[u].astype(jnp.float32)).astype(jnp.bfloat16)
 
             @pl.when(u < SLOTS)
             def _():
@@ -234,7 +248,7 @@
         def _():
             u = s - 1
             p_copy(u).wait_recv()
-            half_out[u] = partial_sum(u, 1 - y).astype(jnp.bfloat16)
+            half_out[u] = partial_sum(u, 1 - finished_by(u)).astype(jnp.bfloat16)
             h_copy(u).start()
 
         @pl.when(s < UNITS)
@@ -320,8 +334,8 @@
         in_specs=[held, held, held, vmem, vmem],
         out_specs=(vmem, vmem, vmem),
         scratch_shapes=[
-            pltpu.VMEM((rows // BLOCK, BLOCK, quarter), b16),
-            pltpu.VMEM((rows // BLOCK, BLOCK, quarter), b16),
+            pltpu.VMEM((2, rows // BLOCK, BLOCK, quarter), b16),
+            pltpu.VMEM((2, rows // BLOCK, BLOCK, quarter), b16),
             pltpu.VMEM((REMOTE, 2, BLOCK, quarter), b16),
             pltpu.VMEM((SLOTS, 2, BLOCK, quarter), b16),
             pltpu.VMEM((UNITS, 2, BLOCK, features), b16),
@@ -331,8 +345,8 @@
             pltpu.VMEM((UNITS, BLOCK, quarter), b16),
             pltpu.VMEM((REMOTE, BLOCK, quarter), b16),
             pltpu.VMEM((UNITS, BLOCK, quarter), b16),
-            pltpu.SMEM(counts.shape, counts.dtype),
-            dma((3 + 2 * SLOTS,)),
+            pltpu.SMEM(counts.shape[::-1], counts.dtype),
+            dma((5 + 2 * SLOTS,)),
             *[dma((REMOTE,))] * 2,
             *[dma((SLOTS,))] * 2,
             *[dma((REMOTE,))] * 6,
@@ -343,7 +357,7 @@
             collective_id=0, has_side_effects=True, vmem_limit_bytes=60 * 1024 * 1024
         ),
     )(
-        counts,
+        counts.T,
         x_rows.reshape(-1, BLOCK, features),
         grad_rows.reshape(-1, BLOCK, features),
         w_gate_up.reshape(2 * units, features),

time: 217 us -> 172 us (0.79)
  Pallas kernels: 208 us -> 164 us
    pallas_call x1, Pallas kernels: 208 us -> 164 us  [on_device(): pl.pallas_call(lambda *refs: kernel(lax.axis_size('blk'), *refs), name='e...]
    unnamed x8 -> x7, local copies, waits for them, and re-layouts: 8.18 us -> 6.79 us
where the time goes in v3:
time: 172 us; the launch traced here: 171 us
  Pallas kernels  164 us (95%)
  local copies, waits for them, and re-layouts  6.79 us (4%)
    pallas_call x1, Pallas kernels, on_device(): pl.pallas_call(lambda *refs: kernel(lax.axis_size('blk'), *refs), name='e...  164 us
    unnamed x7, local copies, waits for them, and re-layouts  6.79 us

profile of v3, /device:TPU:24, one launch (start us, length us, event | category | flops | bytes accessed | tf_op | source)
XLA Modules:
  0.0 171.4 jit_solution(17649916530396508892)
XLA Ops:
  0.6 164.0 %experts_backward.1 = (f32[384,2048]{1,0:T(8,128)}, f32[192,2048]{1,0:T(8,128)}, bf16[1024,512]{1,0:T(8,128)(2,1)}) custom-call(s32[5,64]{1,0:T(8,128)} %bitcast.13, bf16[8,128,2048]{2,1,0:T(8,128)(2,1)} %bitcast.7, bf16[8,128,2048]{2,1,0:T(8,128)(2,1)} %bitcast.8, bf16[384,2048]{1,0:T(8,128)(2,1)} %bitcast.10, bf16[192,2048]{1,0:T(8,128)(2,1)} %bitcast.12), custom_call_target="tpu_custom_call" | custom-call | tf_op jit(solution)/shard_map/experts_backward/pallas_call | solution.py:326
  164.6 0.0 copy-start
  164.7 4.0 %copy.11 = f32[1,2,192,2048]{3,2,1,0:T(8,128)} copy(f32[1,2,192,2048]{3,2,1,0:T(8,128)} %bitcast.9) | data formatting | bytes 6291456
  168.7 0.0 copy-done
  168.7 0.0 copy-start.1
  168.7 1.1 copy.12
  169.8 0.6 copy-done.1
  170.5 1.0 copy.13
Async XLA Ops:
  164.6 4.0 %copy-start = (f32[192,2048]{1,0:T(8,128)S(1)}, f32[192,2048]{1,0:T(8,128)}, u32[]{:S(2)}) copy-start(f32[192,2048]{1,0:T(8,128)} %get-tuple-element.7) | copy-start | bytes 4718596
  168.7 1.8 %copy-start.1 = (bf16[1024,512]{1,0:T(8,128)(2,1)S(1)}, bf16[1024,512]{1,0:T(8,128)(2,1)}, u32[]{:S(2)}) copy-start(bf16[1024,512]{1,0:T(8,128)(2,1)} %get-tuple-element.14) | copy-start | bytes 3145732

commit v4 on v3

--- a/solution.py
+++ b/solution.py
@@ -26,18 +26,22 @@
 HALF_WAY = HOPS
 COLUMN = 8
 HALF = 32
-IN_FLIGHT = 4
+FIRSTS = HOPS
+EXTRAS = 3
 
 
 def offset_of(j):
-    turn, i = j // HOPS, j % HOPS
-    last = turn // (SLOTS - 1)
-    return (1 - last) * (i + 1 + i // 2 - 2 * (i // 3)) + last * (HOPS - i)
-
-
-UNIT_OF = {(offset_of(j), j // HOPS): j for j in range(REMOTE)}
-DIRECT = [j for j in range(REMOTE) if offset_of(j) < HALF_WAY]
-RELAYED = [j for j in range(REMOTE) if offset_of(j) == HALF_WAY]
+    late = (j // FIRSTS + 1) // 2
+    pair = (j - late * FIRSTS) // 2
+    return (1 - late) * (j + 1 + j // 2 - 2 * (j // 3)) + late * (1 + (HOPS - pair) % HOPS)
+
+
+def rank_of(j):
+    return 0 if j < FIRSTS else 1 + j % 2
+
+
+UNIT_OF = {(offset_of(j), rank_of(j)): j for j in range(REMOTE)}
+FAR = UNIT_OF[HALF_WAY, 0]
 
 
 def kernel(
@@ -54,6 +58,10 @@
     g_quarter,
     staged,
     passing,
+    past_1,
+    past_2,
+    past_3,
+    past_4,
     full,
     pieces,
     pieces_in,
@@ -67,6 +75,10 @@
     z_recv,
     n_send,
     n_recv,
+    m_send,
+    m_recv,
+    e_send,
+    e_recv,
     y_send,
     y_recv,
     c_send,
@@ -82,7 +94,7 @@
 ):
     b, y, c = lax.axis_index("blk"), lax.axis_index("dp_0"), lax.axis_index("dp_1")
     unit_count = w_out.shape[0]
-    quarter = x_quarter.shape[3]
+    quarter = x_quarter.shape[2]
 
     def up(position, steps):
         level = lax.rem(position, COLUMN)
@@ -105,10 +117,8 @@
 
     own = cols(y, c)
     loads = []
-    for y_of in range(2):
-        for held, source in ((x_quarter, x_hbm), (g_quarter, g_hbm)):
-            copy = pltpu.make_async_copy(source.at[:, :, cols(y_of, c)], held.at[y_of], load_sem.at[len(loads)])
-            loads.append(copy)
+    for held, source in ((x_quarter, x_hbm), (g_quarter, g_hbm)):
+        loads.append(pltpu.make_async_copy(source.at[:, :, own], held, load_sem.at[len(loads)]))
     for k in range(SLOTS):
         for held, source in ((0, x_hbm), (1, g_hbm)):
             loads.append(pltpu.make_async_copy(source.at[k], full.at[k, held], load_sem.at[len(loads)]))
@@ -123,13 +133,18 @@
     for sender in senders:
         pl.semaphore_signal(barrier, 1, device_id=sender, device_id_type=MESH)
 
-    for load in (*loads[:4], loads[-1]):
+    for load in (*loads[:2], loads[-1]):
         load.wait()
-    live_of = [counts[o, b] for o in range(HOPS + 1)]
-    blocks = [lax.shift_right_logical(n + (BLOCK - 1), 7) for n in live_of]
-    starts = [jnp.int32(0)]
-    for o in range(HOPS):
-        starts.append(starts[o] + blocks[o])
+    def split(position):
+        live = [counts[o, position] for o in range(HOPS + 1)]
+        blocks = [lax.shift_right_logical(n + (BLOCK - 1), 7) for n in live]
+        starts, before = [jnp.int32(0)], [jnp.int32(0)]
+        for o in range(HOPS):
+            starts.append(starts[o] + blocks[o])
+            before.append(before[o] + blocks[o] - 1)
+        return live, blocks, starts, before
+
+    live_of, blocks, starts, before = split(b)
     row_id = lax.broadcasted_iota(jnp.int32, (BLOCK, 1), 0)
 
     def remote(src, dst, send, recv, target):
@@ -137,37 +152,51 @@
             src_ref=src, dst_ref=dst, send_sem=send, recv_sem=recv, device_id=target, device_id_type=MESH
         )
 
+    past = (past_1, past_2, past_3, past_4)
+
     def z_copy(j, target):
-        part = full.at[SLOTS + j, :, :, cols(target[1], c)]
-        return remote(staged.at[j], part, z_send.at[j], z_recv.at[j], target)
-
-    def start_direct(j):
-        z_copy(j, behind(b, offset_of(j))).start()
+        return remote(staged.at[j], full.at[SLOTS + j, :, :, own], z_send.at[j], z_recv.at[j], target)
+
+    def extra_copy(hop, t):
+        source = staged.at[FIRSTS + t] if hop == 0 else past[hop - 1].at[t]
+        at = hop * EXTRAS + t
+        return remote(source, past[hop].at[t], e_send.at[at], e_recv.at[at], behind(b, 1))
 
     def relay_copy(k):
-        j = UNIT_OF[HALF_WAY, k]
-        return remote(staged.at[j], passing.at[k], z_send.at[j], n_recv.at[k], relay_to)
+        source = staged.at[FAR if k == 0 else FIRSTS + k]
+        return remote(source, passing.at[k], n_send.at[k], n_recv.at[k], relay_to)
 
     def pass_copy(k):
-        j = UNIT_OF[HALF_WAY, k]
-        part = full.at[SLOTS + j, :, :, cols(passed_to[1], c)]
-        return remote(passing.at[k], part, n_send.at[k], z_recv.at[j], passed_to)
-
-    for count, j in enumerate(RELAYED[:1] + DIRECT[:1] + RELAYED[1:] + DIRECT[1:]):
-        k, o = j // HOPS, offset_of(j)
-        block = jnp.clip(starts[o] + jnp.minimum(k, blocks[o] - 1), 0, x_quarter.shape[1] - 1)
-        y_of = behind(b, o)[1]
-        staged[j, 0] = x_quarter[y_of, block]
-        live = row_id < live_of[o] - k * BLOCK
-        staged[j, 1] = jnp.where(live, g_quarter[y_of, block], jnp.zeros((), jnp.bfloat16))
-        if count == 0:
+        part = full.at[SLOTS + FAR, :, :, own] if k == 0 else past_4.at[k - 1]
+        landed = z_recv.at[FAR] if k == 0 else m_recv.at[k]
+        return remote(passing.at[k], part, m_send.at[k], landed, passed_to)
+
+    def place(slot, block):
+        block = jnp.clip(block, 0, x_quarter.shape[0] - 1)
+        staged[slot, 0] = x_quarter[block]
+        return g_quarter[block]
+
+    zero = jnp.zeros((), jnp.bfloat16)
+    for j in range(FIRSTS):
+        o = offset_of(j)
+        staged[j, 1] = jnp.where(row_id < live_of[o], place(j, starts[o]), zero)
+        if j == 0:
             pl.semaphore_wait(barrier, len(senders))
         if o == HALF_WAY:
-            relay_copy(k).start()
-        elif j in DIRECT[:IN_FLIGHT]:
-            start_direct(j)
-
-    for load in loads[4:-1]:
+            relay_copy(0).start()
+        else:
+            z_copy(j, behind(b, o)).start()
+    for t in range(EXTRAS):
+        block = jnp.int32(0)
+        for o in range(HOPS + 1):
+            at = t - before[o]
+            block = jnp.where((at >= 0) & (at < blocks[o] - 1), starts[o] + 1 + at, block)
+        staged[FIRSTS + t, 1] = place(FIRSTS + t, block)
+        extra_copy(0, t).start()
+        if t > 0:
+            relay_copy(t).start()
+
+    for load in loads[2:-1]:
         load.wait()
     for k in range(SLOTS):
         live = row_id < live_of[0] - k * BLOCK
@@ -176,16 +205,31 @@
     grad_out[...] = jnp.zeros_like(grad_out)
 
     def y_copy(j):
-        part = full.at[SLOTS + j, :, :, own]
+        part = full.at[SLOTS + j, :, :, cols(ahead(b, offset_of(j))[1], c)]
         return remote(part, part, y_send.at[j], y_recv.at[j], y_peer)
 
     def c_copy(j):
-        part = full.at[SLOTS + j, :, :, own]
+        part = full.at[SLOTS + j, :, :, cols(ahead(b, offset_of(j))[1], c)]
         return remote(part, part, c_send.at[j], c_recv.at[j], c_peer)
 
     def d_copy(j):
-        part = full.at[SLOTS + j, :, :, cols(1 - y, c)]
+        part = full.at[SLOTS + j, :, :, cols(1 - ahead(b, offset_of(j))[1], c)]
         return remote(part, part, d_send.at[j], d_recv.at[j], c_peer)
+
+    def spread(j):
+        y_copy(j).start()
+        c_copy(j).start()
+
+    def pick(j):
+        o, k = offset_of(j), rank_of(j)
+        home_of, y_of, _ = ahead(b, o)
+        live, _, _, first = split(home_of)
+        lowest = 1 if o == HALF_WAY else 0
+        t = jnp.clip(first[o] + k - 1, lowest, EXTRAS - 1) - lowest
+        part = cols(y_of, c)
+        full[SLOTS + j, 0, :, part] = past[o - 1][t, 0]
+        full[SLOTS + j, 1, :, part] = jnp.where(row_id < live[o] - k * BLOCK, past[o - 1][t, 1], zero)
+        spread(j)
 
     def p_copy(u):
         return remote(pieces.at[u, 1 - c], pieces_in.at[u], p_send.at[u], p_recv.at[u], c_peer)
@@ -222,12 +266,11 @@
         return pieces[u, c, y_of].astype(jnp.float32) + pieces_in[u, y_of].astype(jnp.float32)
 
     def step(s, carry):
-        for i, j in enumerate(DIRECT[IN_FLIGHT:]):
-
-            @pl.when(s == i + 2)
-            def _():
-                z_copy(DIRECT[i], y_peer).wait_send()
-                start_direct(j)
+        def forward(at, hop, t):
+            @pl.when(s == at)
+            def _():
+                extra_copy(hop - 1, t).wait_recv()
+                extra_copy(hop, t).start()
 
         @pl.when(s >= 2)
         def _():
@@ -251,6 +294,9 @@
             half_out[u] = partial_sum(u, 1 - finished_by(u)).astype(jnp.bfloat16)
             h_copy(u).start()
 
+        forward(7, 2, 0)
+        forward(8, 2, 1)
+
         @pl.when(s < UNITS)
         def _():
             @pl.when(s >= SLOTS)
@@ -259,6 +305,8 @@
                 d_copy(s - SLOTS).wait_recv()
 
             compute(s)
+
+        forward(8, 2, 2)
 
         @pl.when((s + 1 >= SLOTS) & (s + 1 < UNITS))
         def _():
@@ -273,20 +321,39 @@
                 relay_copy(k).wait_recv()
                 pass_copy(k).start()
 
-        @pl.when((s + 2 >= SLOTS) & (s + 2 < UNITS))
+        @pl.when((s + 2 >= SLOTS) & (s + 2 < SLOTS + FIRSTS))
         def _():
             j = s + 2 - SLOTS
             z_copy(j, y_peer).wait_recv()
-            y_copy(j).start()
-            c_copy(j).start()
+            spread(j)
+
+        forward(4, 1, 0)
+        forward(5, 1, 1)
+        forward(5, 1, 2)
+        for j in range(FIRSTS, REMOTE):
+
+            @pl.when(s + 2 == SLOTS + j)
+            def _():
+                if rank_of(j) == 1 and offset_of(j) == 3:
+                    for t in range(EXTRAS):
+                        extra_copy(2, t).wait_recv()
+                if rank_of(j) == 1 and offset_of(j) == HALF_WAY:
+                    for k in range(1, SLOTS):
+                        pass_copy(k).wait_recv()
+                pick(j)
 
         return carry
 
     lax.fori_loop(0, UNITS + 2, step, 0)
 
-    for j in RELAYED + DIRECT[-IN_FLIGHT:]:
-        z_copy(j, y_peer).wait_send()
+    for j in range(FIRSTS):
+        if j != FAR:
+            z_copy(j, y_peer).wait_send()
+    for hop in range(3):
+        for t in range(EXTRAS):
+            extra_copy(hop, t).wait_send()
     for k in range(SLOTS):
+        relay_copy(k).wait_send()
         pass_copy(k).wait_send()
 
     def drain(j, carry):
@@ -334,10 +401,12 @@
         in_specs=[held, held, held, vmem, vmem],
         out_specs=(vmem, vmem, vmem),
         scratch_shapes=[
-            pltpu.VMEM((2, rows // BLOCK, BLOCK, quarter), b16),
-            pltpu.VMEM((2, rows // BLOCK, BLOCK, quarter), b16),
-            pltpu.VMEM((REMOTE, 2, BLOCK, quarter), b16),
+            pltpu.VMEM((rows // BLOCK, BLOCK, quarter), b16),
+            pltpu.VMEM((rows // BLOCK, BLOCK, quarter), b16),
+            pltpu.VMEM((FIRSTS + EXTRAS, 2, BLOCK, quarter), b16),
             pltpu.VMEM((SLOTS, 2, BLOCK, quarter), b16),
+            *[pltpu.VMEM((EXTRAS, 2, BLOCK, quarter), b16)] * 3,
+            pltpu.VMEM((EXTRAS - 1, 2, BLOCK, quarter), b16),
             pltpu.VMEM((UNITS, 2, BLOCK, features), b16),
             pltpu.VMEM((UNITS, 2, 2, BLOCK, quarter), b16),
             pltpu.VMEM((UNITS, 2, BLOCK, quarter), b16),
@@ -346,9 +415,10 @@
             pltpu.VMEM((REMOTE, BLOCK, quarter), b16),
             pltpu.VMEM((UNITS, BLOCK, quarter), b16),
             pltpu.SMEM(counts.shape[::-1], counts.dtype),
-            dma((5 + 2 * SLOTS,)),
-            *[dma((REMOTE,))] * 2,
-            *[dma((SLOTS,))] * 2,
+            dma((3 + 2 * SLOTS,)),
+            *[dma((FIRSTS,))] * 2,
+            *[dma((SLOTS,))] * 4,
+            *[dma((3 * EXTRAS,))] * 2,
             *[dma((REMOTE,))] * 6,
             *[dma((UNITS,))] * 4,
             *[dma((REMOTE,))] * 2,

time: 172 us -> 179 us (1.041)
  the two profiles are of different devices: /device:TPU:24 before, /device:TPU:32 now
where the time goes in v4:
time: 179 us
  Pallas kernels  171 us (96%)
  local copies, waits for them, and re-layouts  6.79 us (4%)
    pallas_call x1, Pallas kernels, on_device(): pl.pallas_call(lambda *refs: kernel(lax.axis_size('blk'), *refs), name='e...  171 us
    unnamed x7, local copies, waits for them, and re-layouts  6.79 us

profile of v4, /device:TPU:32, one launch (start us, length us, event | category | flops | bytes accessed | tf_op | source)
XLA Modules:
  0.0 178.6 jit_solution(7026130480830837642)
XLA Ops:
  0.6 171.1 %experts_backward.1 = (f32[384,2048]{1,0:T(8,128)}, f32[192,2048]{1,0:T(8,128)}, bf16[1024,512]{1,0:T(8,128)(2,1)}) custom-call(s32[5,64]{1,0:T(8,128)} %bitcast.13, bf16[8,128,2048]{2,1,0:T(8,128)(2,1)} %bitcast.7, bf16[8,128,2048]{2,1,0:T(8,128)(2,1)} %bitcast.8, bf16[384,2048]{1,0:T(8,128)(2,1)} %bitcast.10, bf16[192,2048]{1,0:T(8,128)(2,1)} %bitcast.12), custom_call_target="tpu_custom_call" | custom-call | tf_op jit(solution)/shard_map/experts_backward/pallas_call | solution.py:393
  171.8 0.0 copy-start
  171.8 4.0 %copy.11 = f32[1,2,192,2048]{3,2,1,0:T(8,128)} copy(f32[1,2,192,2048]{3,2,1,0:T(8,128)} %bitcast.9) | data formatting | bytes 6291456
  175.8 0.0 copy-done
  175.8 0.0 copy-start.1
  175.8 1.1 copy.12
  176.9 0.6 copy-done.1
  177.6 1.0 copy.13
Async XLA Ops:
  171.8 4.0 %copy-start = (f32[192,2048]{1,0:T(8,128)S(1)}, f32[192,2048]{1,0:T(8,128)}, u32[]{:S(2)}) copy-start(f32[192,2048]{1,0:T(8,128)} %get-tuple-element.7) | copy-start | bytes 4718596
  175.8 1.8 %copy-start.1 = (bf16[1024,512]{1,0:T(8,128)(2,1)S(1)}, bf16[1024,512]{1,0:T(8,128)(2,1)}, u32[]{:S(2)}) copy-start(bf16[1024,512]{1,0:T(8,128)(2,1)} %get-tuple-element.14) | copy-start | bytes 3145732

commit v5 on v4

--- a/solution.py
+++ b/solution.py
@@ -31,16 +31,14 @@
 
 
 def offset_of(j):
-    late = (j // FIRSTS + 1) // 2
-    pair = (j - late * FIRSTS) // 2
-    return (1 - late) * (j + 1 + j // 2 - 2 * (j // 3)) + late * (1 + (HOPS - pair) % HOPS)
-
-
-def rank_of(j):
-    return 0 if j < FIRSTS else 1 + j % 2
-
-
-UNIT_OF = {(offset_of(j), rank_of(j)): j for j in range(REMOTE)}
+    def since(first):
+        return (j + REMOTE - first) // REMOTE
+
+    return 1 + 3 * since(1) - 3 * since(2) + since(4) + 2 * since(7) - since(9)
+
+
+RANKS = (0, 0, 1, 2, 0, 1, 2, 1, 2, 0, 1, 2)
+UNIT_OF = {(offset_of(j), RANKS[j]): j for j in range(REMOTE)}
 FAR = UNIT_OF[HALF_WAY, 0]
 
 
@@ -154,8 +152,9 @@
 
     past = (past_1, past_2, past_3, past_4)
 
-    def z_copy(j, target):
-        return remote(staged.at[j], full.at[SLOTS + j, :, :, own], z_send.at[j], z_recv.at[j], target)
+    def z_copy(o):
+        part = full.at[SLOTS + UNIT_OF[o, 0], :, :, own]
+        return remote(staged.at[o - 1], part, z_send.at[o - 1], z_recv.at[o - 1], behind(b, o))
 
     def extra_copy(hop, t):
         source = staged.at[FIRSTS + t] if hop == 0 else past[hop - 1].at[t]
@@ -163,12 +162,12 @@
         return remote(source, past[hop].at[t], e_send.at[at], e_recv.at[at], behind(b, 1))
 
     def relay_copy(k):
-        source = staged.at[FAR if k == 0 else FIRSTS + k]
+        source = staged.at[HALF_WAY - 1 if k == 0 else FIRSTS + k]
         return remote(source, passing.at[k], n_send.at[k], n_recv.at[k], relay_to)
 
     def pass_copy(k):
         part = full.at[SLOTS + FAR, :, :, own] if k == 0 else past_4.at[k - 1]
-        landed = z_recv.at[FAR] if k == 0 else m_recv.at[k]
+        landed = z_recv.at[HALF_WAY - 1] if k == 0 else m_recv.at[k]
         return remote(passing.at[k], part, m_send.at[k], landed, passed_to)
 
     def place(slot, block):
@@ -177,15 +176,14 @@
         return g_quarter[block]
 
     zero = jnp.zeros((), jnp.bfloat16)
-    for j in range(FIRSTS):
-        o = offset_of(j)
-        staged[j, 1] = jnp.where(row_id < live_of[o], place(j, starts[o]), zero)
-        if j == 0:
-            pl.semaphore_wait(barrier, len(senders))
-        if o == HALF_WAY:
-            relay_copy(0).start()
-        else:
-            z_copy(j, behind(b, o)).start()
+    def place_first(o):
+        staged[o - 1, 1] = jnp.where(row_id < live_of[o], place(o - 1, starts[o]), zero)
+
+    place_first(1)
+    pl.semaphore_wait(barrier, len(senders))
+    z_copy(1).start()
+    place_first(HALF_WAY)
+    relay_copy(0).start()
     for t in range(EXTRAS):
         block = jnp.int32(0)
         for o in range(HOPS + 1):
@@ -193,8 +191,8 @@
             block = jnp.where((at >= 0) & (at < blocks[o] - 1), starts[o] + 1 + at, block)
         staged[FIRSTS + t, 1] = place(FIRSTS + t, block)
         extra_copy(0, t).start()
-        if t > 0:
-            relay_copy(t).start()
+    place_first(2)
+    place_first(3)
 
     for load in loads[2:-1]:
         load.wait()
@@ -221,7 +219,7 @@
         c_copy(j).start()
 
     def pick(j):
-        o, k = offset_of(j), rank_of(j)
+        o, k = offset_of(j), RANKS[j]
         home_of, y_of, _ = ahead(b, o)
         live, _, _, first = split(home_of)
         lowest = 1 if o == HALF_WAY else 0
@@ -272,6 +270,20 @@
                 extra_copy(hop - 1, t).wait_recv()
                 extra_copy(hop, t).start()
 
+        def relay(at, k):
+            @pl.when(s == at)
+            def _():
+                relay_copy(k).wait_recv()
+                pass_copy(k).start()
+                if k == 0:
+                    relay_copy(1).start()
+                    relay_copy(2).start()
+
+        def start_first(at, o):
+            @pl.when(s == at)
+            def _():
+                z_copy(o).start()
+
         @pl.when(s >= 2)
         def _():
             u = s - 2
@@ -294,9 +306,6 @@
             half_out[u] = partial_sum(u, 1 - finished_by(u)).astype(jnp.bfloat16)
             h_copy(u).start()
 
-        forward(7, 2, 0)
-        forward(8, 2, 1)
-
         @pl.when(s < UNITS)
         def _():
             @pl.when(s >= SLOTS)
@@ -306,7 +315,10 @@
 
             compute(s)
 
-        forward(8, 2, 2)
+        forward(3, 1, 2)
+        relay(3, 2)
+        forward(5, 2, 0)
+        forward(6, 2, 1)
 
         @pl.when((s + 1 >= SLOTS) & (s + 1 < UNITS))
         def _():
@@ -314,41 +326,36 @@
             y_copy(j).wait_recv()
             d_copy(j).start()
 
-        for k in range(SLOTS):
-
-            @pl.when(s == k)
-            def _():
-                relay_copy(k).wait_recv()
-                pass_copy(k).start()
-
-        @pl.when((s + 2 >= SLOTS) & (s + 2 < SLOTS + FIRSTS))
-        def _():
-            j = s + 2 - SLOTS
-            z_copy(j, y_peer).wait_recv()
-            spread(j)
-
-        forward(4, 1, 0)
-        forward(5, 1, 1)
-        forward(5, 1, 2)
-        for j in range(FIRSTS, REMOTE):
+        relay(0, 0)
+        forward(2, 1, 0)
+        forward(2, 1, 1)
+        relay(2, 1)
+        forward(6, 2, 2)
+        for j in range(REMOTE):
+            o, k = offset_of(j), RANKS[j]
 
             @pl.when(s + 2 == SLOTS + j)
             def _():
-                if rank_of(j) == 1 and offset_of(j) == 3:
+                if k == 0:
+                    (pass_copy(0) if o == HALF_WAY else z_copy(o)).wait_recv()
+                    spread(j)
+                elif k == 1 and o == 3:
                     for t in range(EXTRAS):
                         extra_copy(2, t).wait_recv()
-                if rank_of(j) == 1 and offset_of(j) == HALF_WAY:
-                    for k in range(1, SLOTS):
-                        pass_copy(k).wait_recv()
-                pick(j)
-
+                elif k == 1 and o == HALF_WAY:
+                    for extra in range(1, EXTRAS):
+                        pass_copy(extra).wait_recv()
+                if k > 0:
+                    pick(j)
+
+        start_first(1, 2)
+        start_first(3, 3)
         return carry
 
     lax.fori_loop(0, UNITS + 2, step, 0)
 
-    for j in range(FIRSTS):
-        if j != FAR:
-            z_copy(j, y_peer).wait_send()
+    for o in range(1, HALF_WAY):
+        z_copy(o).wait_send()
     for hop in range(3):
         for t in range(EXTRAS):
             extra_copy(hop, t).wait_send()

time: 179 us -> 180 us (level)
  the two profiles are of different devices: /device:TPU:32 before, /device:TPU:72 now
where the time goes in v5:
time: 180 us
  Pallas kernels  172 us (96%)
  local copies, waits for them, and re-layouts  6.79 us (4%)
    pallas_call x1, Pallas kernels, on_device(): pl.pallas_call(lambda *refs: kernel(lax.axis_size('blk'), *refs), name='e...  172 us
    unnamed x7, local copies, waits for them, and re-layouts  6.79 us

profile of v5, /device:TPU:72, one launch (start us, length us, event | category | flops | bytes accessed | tf_op | source)
XLA Modules:
  0.0 179.8 jit_solution(2411959555326076228)
XLA Ops:
  0.6 172.4 %experts_backward.1 = (f32[384,2048]{1,0:T(8,128)}, f32[192,2048]{1,0:T(8,128)}, bf16[1024,512]{1,0:T(8,128)(2,1)}) custom-call(s32[5,64]{1,0:T(8,128)} %bitcast.13, bf16[8,128,2048]{2,1,0:T(8,128)(2,1)} %bitcast.7, bf16[8,128,2048]{2,1,0:T(8,128)(2,1)} %bitcast.8, bf16[384,2048]{1,0:T(8,128)(2,1)} %bitcast.10, bf16[192,2048]{1,0:T(8,128)(2,1)} %bitcast.12), custom_call_target="tpu_custom_call" | custom-call | tf_op jit(solution)/shard_map/experts_backward/pallas_call | solution.py:400
  173.0 0.0 copy-start
  173.0 4.0 %copy.11 = f32[1,2,192,2048]{3,2,1,0:T(8,128)} copy(f32[1,2,192,2048]{3,2,1,0:T(8,128)} %bitcast.9) | data formatting | bytes 6291456
  177.1 0.0 copy-done
  177.1 0.0 copy-start.1
  177.1 1.1 copy.12
  178.2 0.6 copy-done.1
  178.9 1.0 copy.13
Async XLA Ops:
  173.0 4.0 %copy-start = (f32[192,2048]{1,0:T(8,128)S(1)}, f32[192,2048]{1,0:T(8,128)}, u32[]{:S(2)}) copy-start(f32[192,2048]{1,0:T(8,128)} %get-tuple-element.7) | copy-start | bytes 4718596
  177.1 1.8 copy-start.1

commit v6 on v5

--- a/solution.py
+++ b/solution.py
@@ -315,10 +315,10 @@
 
             compute(s)
 
-        forward(3, 1, 2)
-        relay(3, 2)
-        forward(5, 2, 0)
-        forward(6, 2, 1)
+        forward(2, 1, 2)
+        relay(2, 2)
+        forward(4, 2, 0)
+        forward(5, 2, 1)
 
         @pl.when((s + 1 >= SLOTS) & (s + 1 < UNITS))
         def _():
@@ -327,14 +327,14 @@
             d_copy(j).start()
 
         relay(0, 0)
-        forward(2, 1, 0)
-        forward(2, 1, 1)
-        relay(2, 1)
-        forward(6, 2, 2)
+        forward(1, 1, 0)
+        forward(1, 1, 1)
+        relay(1, 1)
+        forward(5, 2, 2)
         for j in range(REMOTE):
             o, k = offset_of(j), RANKS[j]
 
-            @pl.when(s + 2 == SLOTS + j)
+            @pl.when(s + 3 == SLOTS + j)
             def _():
                 if k == 0:
                     (pass_copy(0) if o == HALF_WAY else z_copy(o)).wait_recv()
@@ -348,8 +348,8 @@
                 if k > 0:
                     pick(j)
 
-        start_first(1, 2)
-        start_first(3, 3)
+        start_first(0, 2)
+        start_first(2, 3)
         return carry
 
     lax.fori_loop(0, UNITS + 2, step, 0)

time: 180 us -> 186 us (1.033)
  Pallas kernels: 172 us -> 178 us
    pallas_call x1, Pallas kernels: 172 us -> 178 us  [on_device(): pl.pallas_call(lambda *refs: kernel(lax.axis_size('blk'), *refs), name='e...]
where the time goes in v6:
time: 186 us
  Pallas kernels  178 us (96%)
  local copies, waits for them, and re-layouts  6.79 us (4%)
    pallas_call x1, Pallas kernels, on_device(): pl.pallas_call(lambda *refs: kernel(lax.axis_size('blk'), *refs), name='e...  178 us
    unnamed x7, local copies, waits for them, and re-layouts  6.79 us

profile of v6, /device:TPU:72, one launch (start us, length us, event | category | flops | bytes accessed | tf_op | source)
XLA Modules:
  0.0 185.9 jit_solution(7412114069529280950)
XLA Ops:
  0.6 178.5 %experts_backward.1 = (f32[384,2048]{1,0:T(8,128)}, f32[192,2048]{1,0:T(8,128)}, bf16[1024,512]{1,0:T(8,128)(2,1)}) custom-call(s32[5,64]{1,0:T(8,128)} %bitcast.13, bf16[8,128,2048]{2,1,0:T(8,128)(2,1)} %bitcast.7, bf16[8,128,2048]{2,1,0:T(8,128)(2,1)} %bitcast.8, bf16[384,2048]{1,0:T(8,128)(2,1)} %bitcast.10, bf16[192,2048]{1,0:T(8,128)(2,1)} %bitcast.12), custom_call_target="tpu_custom_call" | custom-call | tf_op jit(solution)/shard_map/experts_backward/pallas_call | solution.py:400
  179.1 0.0 copy-start
  179.1 4.0 %copy.11 = f32[1,2,192,2048]{3,2,1,0:T(8,128)} copy(f32[1,2,192,2048]{3,2,1,0:T(8,128)} %bitcast.9) | data formatting | bytes 6291456
  183.2 0.0 copy-done
  183.2 0.0 copy-start.1
  183.2 1.1 copy.12
  184.3 0.6 copy-done.1
  185.0 1.0 copy.13
Async XLA Ops:
  179.1 4.0 %copy-start = (f32[192,2048]{1,0:T(8,128)S(1)}, f32[192,2048]{1,0:T(8,128)}, u32[]{:S(2)}) copy-start(f32[192,2048]{1,0:T(8,128)} %get-tuple-element.7) | copy-start | bytes 4718596
  183.2 1.8 copy-start.1

commit v7 on v3

--- a/solution.py
+++ b/solution.py
@@ -26,7 +26,7 @@
 HALF_WAY = HOPS
 COLUMN = 8
 HALF = 32
-IN_FLIGHT = 4
+IN_FLIGHT = 3
 
 
 def offset_of(j):
@@ -47,9 +47,14 @@
     g_hbm,
     w_in,
     w_out,
+    grad_in_hbm,
+    grad_out_hbm,
+    grad_x,
     grad_in,
     grad_out,
-    grad_x,
+    both_of,
+    hidden_of,
+    store_sem,
     x_quarter,
     g_quarter,
     staged,
@@ -215,11 +220,23 @@
                 both, w_in[:, q * quarter : (q + 1) * quarter], preferred_element_type=jnp.float32
             ).astype(jnp.bfloat16)
         p_copy(u).start()
-        grad_in[...] += contract_first(both, rows_in)
-        grad_out[...] += contract_first(hidden, rows_cot)
+        both_of[...] = both
+        hidden_of[...] = hidden
+
+    def add_grads(u):
+        grad_in[...] += contract_first(both_of[...], full[u, 0])
+        grad_out[...] += contract_first(hidden_of[...], full[u, 1])
 
     def partial_sum(u, y_of):
         return pieces[u, c, y_of].astype(jnp.float32) + pieces_in[u, y_of].astype(jnp.float32)
+
+    def finished(u):
+        h_copy(u).wait_recv()
+        return (partial_sum(u, finished_by(u)) + half_in[u].astype(jnp.float32)).astype(jnp.bfloat16)
+
+    def send_home(j, total):
+        home_out[j] = total
+        r_copy(j).start()
 
     def step(s, carry):
         for i, j in enumerate(DIRECT[IN_FLIGHT:]):
@@ -232,8 +249,7 @@
         @pl.when(s >= 2)
         def _():
             u = s - 2
-            h_copy(u).wait_recv()
-            total = (partial_sum(u, finished_by(u)) + half_in[u].astype(jnp.float32)).astype(jnp.bfloat16)
+            total = finished(u)
 
             @pl.when(u < SLOTS)
             def _():
@@ -241,8 +257,7 @@
 
             @pl.when(u >= SLOTS)
             def _():
-                home_out[u - SLOTS] = total
-                r_copy(u - SLOTS).start()
+                send_home(u - SLOTS, total)
 
         @pl.when((s >= 1) & (s < UNITS + 1))
         def _():
@@ -250,6 +265,7 @@
             p_copy(u).wait_recv()
             half_out[u] = partial_sum(u, 1 - finished_by(u)).astype(jnp.bfloat16)
             h_copy(u).start()
+            add_grads(u)
 
         @pl.when(s < UNITS)
         def _():
@@ -282,7 +298,14 @@
 
         return carry
 
-    lax.fori_loop(0, UNITS + 2, step, 0)
+    lax.fori_loop(0, UNITS + 1, step, 0)
+    stores = [
+        pltpu.make_async_copy(grad_in, grad_in_hbm, store_sem.at[0]),
+        pltpu.make_async_copy(grad_out, grad_out_hbm, store_sem.at[1]),
+    ]
+    for store in stores:
+        store.start()
+    send_home(REMOTE - 1, finished(UNITS - 1))
 
     for j in RELAYED + DIRECT[-IN_FLIGHT:]:
         z_copy(j, y_peer).wait_send()
@@ -305,6 +328,8 @@
         return carry
 
     lax.fori_loop(0, UNITS, drain_sums, 0)
+    for store in stores:
+        store.wait()
 
     for p in range(grad_x.shape[0] // BLOCK):
         unit = jnp.int32(0)
@@ -332,8 +357,13 @@
             jax.ShapeDtypeStruct((rows, quarter), b16),
         ),
         in_specs=[held, held, held, vmem, vmem],
-        out_specs=(vmem, vmem, vmem),
+        out_specs=(held, held, vmem),
         scratch_shapes=[
+            pltpu.VMEM((2 * units, features), f32),
+            pltpu.VMEM((units, features), f32),
+            pltpu.VMEM((BLOCK, 2 * units), b16),
+            pltpu.VMEM((BLOCK, units), b16),
+            dma((2,)),
             pltpu.VMEM((2, rows // BLOCK, BLOCK, quarter), b16),
             pltpu.VMEM((2, rows // BLOCK, BLOCK, quarter), b16),
             pltpu.VMEM((REMOTE, 2, BLOCK, quarter), b16),

time: 172 us -> 168 us (0.977)
  Pallas kernels: 164 us -> 160 us
    pallas_call x1, Pallas kernels: 164 us -> 160 us  [on_device(): pl.pallas_call(lambda *refs: kernel(lax.axis_size('blk'), *refs), name='e...]
where the time goes in v7:
time: 168 us; the launch traced here: 167 us
  Pallas kernels  160 us (95%)
  local copies, waits for them, and re-layouts  6.79 us (4%)
    pallas_call x1, Pallas kernels, on_device(): pl.pallas_call(lambda *refs: kernel(lax.axis_size('blk'), *refs), name='e...  160 us
    unnamed x7, local copies, waits for them, and re-layouts  6.79 us

profile of v7, /device:TPU:24, one launch (start us, length us, event | category | flops | bytes accessed | tf_op | source)
XLA Modules:
  0.0 167.4 jit_solution(15986827226883981520)
XLA Ops:
  0.6 160.0 %experts_backward.1 = (f32[384,2048]{1,0:T(8,128)}, f32[192,2048]{1,0:T(8,128)}, bf16[1024,512]{1,0:T(8,128)(2,1)}) custom-call(s32[5,64]{1,0:T(8,128)} %bitcast.13, bf16[8,128,2048]{2,1,0:T(8,128)(2,1)} %bitcast.7, bf16[8,128,2048]{2,1,0:T(8,128)(2,1)} %bitcast.8, bf16[384,2048]{1,0:T(8,128)(2,1)} %bitcast.10, bf16[192,2048]{1,0:T(8,128)(2,1)} %bitcast.12), custom_call_target="tpu_custom_call" | custom-call | tf_op jit(solution)/shard_map/experts_backward/pallas_call | solution.py:351
  160.6 0.0 copy-start
  160.6 4.0 %copy.11 = f32[1,2,192,2048]{3,2,1,0:T(8,128)} copy(f32[1,2,192,2048]{3,2,1,0:T(8,128)} %bitcast.9) | data formatting | bytes 6291456
  164.6 0.0 copy-done
  164.6 0.0 copy-start.1
  164.6 1.1 copy.12
  165.8 0.6 copy-done.1
  166.4 1.0 copy.13
Async XLA Ops:
  160.6 4.0 %copy-start = (f32[192,2048]{1,0:T(8,128)S(1)}, f32[192,2048]{1,0:T(8,128)}, u32[]{:S(2)}) copy-start(f32[192,2048]{1,0:T(8,128)} %get-tuple-element.7) | copy-start | bytes 4718596
  164.6 1.8 %copy-start.1 = (bf16[1024,512]{1,0:T(8,128)(2,1)S(1)}, bf16[1024,512]{1,0:T(8,128)(2,1)}, u32[]{:S(2)}) copy-start(bf16[1024,512]{1,0:T(8,128)(2,1)} %get-tuple-element.14) | copy-start | bytes 3145732
